TPU v7x, 512 devices: a whole 4x8x8 slice. The times are simulated.
512 devices in a mesh: stu: 16 (over z_lo, x), que: 32 (over z_hi, y, core).
Axes of the slice: x: 4, y: 8, z: 8 (z_hi: 2, z_lo: 4; z = z_hi * 4 + z_lo), core: 2. Of those that a mesh axis runs over, the one named last changes fastest.
Arguments:
- codes: int32 [4096, 4096], P('stu', 'que'), may hold values from 0 to 2
- theta: float32 [4096, 64], P(('stu', 'que')), may hold values from -6 to 6
- disc: float32 [4096, 64], P(('que', 'stu')), may hold values from -0.75 to 0.75
- intercept: float32 [4096], P(('que', 'stu')), may hold values from -5 to 5
Outputs:
- step_abilities: float32 [4096, 64], P(('stu', 'que'))
- step_disc: float32 [4096, 64], P(('que', 'stu'))
- step_intercept: float32 [4096], P(('que', 'stu'))
All inputs are finite; a program needn't handle non-finite values.
Results may differ from a plain program's by a relative error of at most 0.0003.
Values sent between devices are 32-bit elements; how exact they have to be, the bound alone decides.
A program may use at most 64 MiB of HBM per device.

v0:
```python
import jax
import jax.numpy as jnp
from jax import lax
from jax.sharding import PartitionSpec as P

ITERS = 2


HIGH = lax.Precision.HIGHEST


def matmul(left, right):
    return jnp.dot(left, right, precision=HIGH, preferred_element_type=jnp.float32)


def contract_rows(left, right):
    return lax.dot_general(
        left, right, (((0,), (0,)), ((), ())), precision=HIGH, preferred_element_type=jnp.float32
    )


def local_inner(left, right):
    return jnp.sum(left[0] * right[0]) + jnp.sum(left[1] * right[1]) + jnp.sum(left[2] * right[2])


def squared(residual, precond):
    return lax.psum(local_inner(residual, precond), ("stu", "que"))


def combine(first, factor, second):
    return jax.tree.map(lambda u, v: u + factor * v, first, second)


def shards(codes, theta, disc, intercept):
    theta_rows = lax.all_gather(theta, "que", axis=0, tiled=True)
    disc_cols, icpt_cols = (
        lax.all_gather(disc, "stu", axis=0, tiled=True),
        lax.all_gather(intercept, "stu", axis=0, tiled=True),
    )
    logit = matmul(theta_rows, disc_cols.T) + icpt_cols[None, :]
    prob = jax.nn.sigmoid(logit)
    observed = (codes > 0).astype(jnp.float32)
    correct = (codes == 2).astype(jnp.float32)
    resid = observed * (prob - correct)
    weight = observed * prob * (1.0 - prob)
    row_one = matmul(resid, disc_cols)
    row_two = matmul(weight, disc_cols * disc_cols)
    col_one = contract_rows(resid, theta_rows)
    col_two = contract_rows(weight, theta_rows * theta_rows)
    col_three = jnp.sum(resid, 0)
    col_four = jnp.sum(weight, 0)
    row_sum = (
        lax.psum_scatter(row_one, "que", scatter_dimension=0, tiled=True),
        lax.psum_scatter(row_two, "que", scatter_dimension=0, tiled=True),
    )
    col_sum = (
        lax.psum_scatter(col_one, "stu", scatter_dimension=0, tiled=True),
        lax.psum_scatter(col_two, "stu", scatter_dimension=0, tiled=True),
        lax.psum_scatter(col_three, "stu", scatter_dimension=0, tiled=True),
        lax.psum_scatter(col_four, "stu", scatter_dimension=0, tiled=True),
    )
    own = (theta, disc, intercept)
    grad = (row_sum[0] + own[0], col_sum[0] + own[1], col_sum[2] + own[2])
    diag = (row_sum[1] + 1.0, col_sum[1] + 1.0, col_sum[3] + 1.0)
    solution = jax.tree.map(jnp.zeros_like, grad)
    residual = jax.tree.map(lambda u: -u, grad)
    precond = jax.tree.map(lambda u, d: u / d, residual, diag)
    direction = precond
    norm_now = squared(residual, precond)
    for step in range(ITERS):
        vt_rows = lax.all_gather(direction[0], "que", axis=0, tiled=True)
        va_cols = lax.all_gather(direction[1], "stu", axis=0, tiled=True)
        vb_cols = lax.all_gather(direction[2], "stu", axis=0, tiled=True)
        left = jnp.concatenate([vt_rows, theta_rows], 1)
        right = jnp.concatenate([disc_cols, va_cols], 1)
        change = matmul(left, right.T) + vb_cols[None, :]
        scaled = weight * change
        part_rows = matmul(scaled, disc_cols)
        part_disc = contract_rows(scaled, theta_rows)
        part_icpt = jnp.sum(scaled, 0)
        summed_rows = lax.psum_scatter(part_rows, "que", scatter_dimension=0, tiled=True)
        summed_disc = lax.psum_scatter(part_disc, "stu", scatter_dimension=0, tiled=True)
        summed_icpt = lax.psum_scatter(part_icpt, "stu", scatter_dimension=0, tiled=True)
        image = (summed_rows + direction[0], summed_disc + direction[1], summed_icpt + direction[2])
        alpha = norm_now / lax.psum(local_inner(direction, image), ("stu", "que"))
        solution = combine(solution, alpha, direction)
        residual = combine(residual, -alpha, image)
        if step + 1 < ITERS:
            precond = jax.tree.map(lambda u, d: u / d, residual, diag)
            norm_next = squared(residual, precond)
            ratio = norm_next / norm_now
            direction = combine(precond, ratio, direction)
            norm_now = norm_next
    result = jax.tree.map(lambda u, d: u * jnp.sqrt(d), solution, diag)
    return (result[0], result[1], result[2])


def solution(mesh):
    placed = (P("stu", "que"), P(("stu", "que"), None), P(("que", "stu"), None), P(("que", "stu")))
    return jax.shard_map(
        shards,
        mesh=mesh,
        in_specs=placed,
        out_specs=(P(("stu", "que"), None), P(("que", "stu"), None), P(("que", "stu"))),
        check_vma=False,
    )
```

profile of v0, /device:TPU:1, one launch (start us, length us, event | category | flops | bytes accessed | tf_op | source)
XLA Modules:
  0.0 1810.6 jit_solution(3583325412611648461)
XLA Ops:
  7.2 60.0 %all_gather.27 = f32[256,64]{1,0:T(8,128)S(1)} all-gather(f32[8,64]{1,0:T(8,128)} %param.5), channel_id=1, replica_groups=mesh['stu'=16,'que'=32] {'que'}, dimensions={0}, use_global_device_ids=true | all-gather | bytes 67584 | tf_op jit(solution)/shard_map/all_gather | solution.py:35
  69.4 36.2 %all-reduce = f32[128]{0:T(128)S(1)} all-reduce(f32[128]{0:T(128)S(1)} %dynamic-update-slice), channel_id=1, replica_groups=mesh['stu'=16,'que'=32] {'stu'}, use_global_device_ids=true, to_apply=%add | all-reduce | flops 128 | bytes 1024
  105.6 30.4 %all_gather.28 = f32[128,64]{1,0:T(8,128)S(1)} all-gather(f32[8,64]{1,0:T(8,128)S(1)} %copy-done.1), channel_id=1, replica_groups=mesh['stu'=16,'que'=32] {'stu'}, dimensions={0}, use_global_device_ids=true | all-gather | bytes 34816 | tf_op jit(solution)/shard_map/all_gather | solution.py:37
  138.4 32.3 %all-reduce.20 = (f32[128]{0:T(128)S(1)}, f32[128]{0:T(128)S(1)}) all-reduce(f32[128]{0:T(128)S(1)} %get-tuple-element.35, f32[128]{0:T(128)S(1)} %get-tuple-element.31), channel_id=6, replica_groups=mesh['stu'=16,'que'=32] {'stu'}, use_global_device_ids=true, to_apply=%region_7.0.clone | all-reduce | flops 256 | bytes 2048
  174.0 1.3 dynamic-slice.3
  176.0 152.3 %all-reduce.32.cloned.1.call-done = (f32[128,64]{1,0:T(8,128)}, f32[128,64]{1,0:T(8,128)}, f32[128]{0:T(128)}) async-done(((f32[128,64]{1,0:T(8,128)}, f32[128,64]{1,0:T(8,128)}, f32[128]{0:T(128)}), (f32[128,64]{1,0:T(8,128)}, f32[128,64]{1,0:T(8,128)}, f32[128]{0:T(128)})) %all-reduce.32.cloned.1.call-update) | async-done | bytes 66064
  328.9 35.5 %all_gather.31 = f32[128,64]{1,0:T(8,128)S(1)} all-gather(f32[8,64]{1,0:T(8,128)S(1)} %get-tuple-element.26), channel_id=1, replica_groups=mesh['stu'=16,'que'=32] {'stu'}, dimensions={0}, use_global_device_ids=true | all-gather | bytes 34816 | tf_op jit(solution)/shard_map/all_gather | solution.py:72
  364.4 318.1 %all-reduce.30.cloned.1.call-done = (f32[256,64]{1,0:T(8,128)}, f32[256,64]{1,0:T(8,128)}) async-done(((f32[256,64]{1,0:T(8,128)}, f32[256,64]{1,0:T(8,128)}), (f32[256,64]{1,0:T(8,128)}, f32[256,64]{1,0:T(8,128)})) %all-reduce.30.cloned.1.call-update) | async-done | bytes 131088
  683.2 47.3 %all_gather.30 = f32[256,64]{1,0:T(8,128)S(1)} all-gather(f32[8,64]{1,0:T(8,128)S(1)} %get-tuple-element.33), channel_id=1, replica_groups=mesh['stu'=16,'que'=32] {'que'}, dimensions={0}, use_global_device_ids=true | all-gather | bytes 67584 | tf_op jit(solution)/shard_map/all_gather | solution.py:71
  733.0 67.3 %all-reduce.18 = (f32[128,64]{1,0:T(8,128)S(1)}, f32[128]{0:T(128)S(1)}) all-reduce(f32[128,64]{1,0:T(8,128)S(1)} %fusion.51, f32[128]{0:T(128)S(1)} %get-tuple-element.39), channel_id=9, replica_groups=mesh['stu'=16,'que'=32] {'stu'}, use_global_device_ids=true, to_apply=%region_14.0.clone | all-reduce | flops 8320 | bytes 66560
  801.7 247.6 %all-reduce.26.cloned.1.call-done = f32[256,64]{1,0:T(8,128)} async-done(((f32[256,64]{1,0:T(8,128)}), f32[256,64]{1,0:T(8,128)}) %all-reduce.26.cloned.1.call-update) | async-done | bytes 65552
  1049.3 1.3 multiply_reduce_fusion.3
  1054.4 98.3 %all-reduce.15 = (f32[]{:T(128)}, f32[]{:T(128)}) all-reduce(f32[]{:T(128)S(6)} %add.156, f32[]{:T(128)S(6)} %add.163), channel_id=1, replica_groups=mesh['stu'=16,'que'=32] {'stu','que'}, use_global_device_ids=true, to_apply=%region_11.0 | all-reduce | flops 2 | bytes 16 | tf_op jit(solution)/shard_map/psum | solution.py:27
  1154.1 1.4 multiply_reduce_fusion
  1156.1 1.3 multiply_reduce_fusion.1
  1159.3 94.4 %psum.30 = f32[]{:T(128)} all-reduce(f32[]{:T(128)S(6)} %add.168), channel_id=1, replica_groups=mesh['stu'=16,'que'=32] {'stu','que'}, use_global_device_ids=true, to_apply=%region_23.0 | all-reduce | flops 1 | bytes 8 | tf_op jit(solution)/shard_map/psum | solution.py:27
  1255.8 34.9 %all-reduce.2 = f32[128]{0:T(128)S(1)} all-reduce(f32[128]{0:T(128)S(1)} %get-tuple-element.22), channel_id=1, replica_groups=mesh['stu'=16,'que'=32] {'stu'}, use_global_device_ids=true, to_apply=%add.2 | all-reduce | flops 128 | bytes 1024
  1290.8 30.4 %all_gather.34 = f32[128,64]{1,0:T(8,128)S(1)} all-gather(f32[8,64]{1,0:T(8,128)S(1)} %multiply_add_fusion), channel_id=1, replica_groups=mesh['stu'=16,'que'=32] {'stu'}, dimensions={0}, use_global_device_ids=true | all-gather | bytes 34816 | tf_op jit(solution)/shard_map/all_gather | solution.py:72
  1321.9 63.4 %all_gather.33 = f32[256,64]{1,0:T(8,128)S(1)} all-gather(f32[8,64]{1,0:T(8,128)S(1)} %multiply_add_fusion.1), channel_id=1, replica_groups=mesh['stu'=16,'que'=32] {'que'}, dimensions={0}, use_global_device_ids=true | all-gather | bytes 67584 | tf_op jit(solution)/shard_map/all_gather | solution.py:71
  1387.0 64.5 %all-reduce.17 = (f32[128,64]{1,0:T(8,128)S(1)}, f32[128]{0:T(128)S(1)}) all-reduce(f32[128,64]{1,0:T(8,128)S(1)} %fusion.53, f32[128]{0:T(128)S(1)} %get-tuple-element.41), channel_id=12, replica_groups=mesh['stu'=16,'que'=32] {'stu'}, use_global_device_ids=true, to_apply=%region_26.0.clone | all-reduce | flops 8320 | bytes 66560
  1452.8 246.5 %all-reduce.28.cloned.1.call-done = f32[256,64]{1,0:T(8,128)} async-done(((f32[256,64]{1,0:T(8,128)}), f32[256,64]{1,0:T(8,128)}) %all-reduce.28.cloned.1.call-update) | async-done | bytes 65552
  1699.3 1.3 fusion.22
  1702.5 98.3 %psum.31 = f32[]{:T(128)} all-reduce(f32[]{:T(128)S(6)} %add.178), channel_id=1, replica_groups=mesh['stu'=16,'que'=32] {'stu','que'}, use_global_device_ids=true, to_apply=%region_31.0 | all-reduce | flops 1 | bytes 8 | tf_op jit(solution)/shard_map/psum | solution.py:85
  1802.2 1.3 sqrt_multiply_fusion
  (50 shorter events, 17.6 us)
Async XLA Ops:
  7.2 128.9 %copy-start = (s32[256,128]{1,0:T(8,128)S(1)}, s32[256,128]{1,0:T(8,128)}, u32[]{:S(2)}) copy-start(s32[256,128]{1,0:T(8,128)} %param.4) | copy-start | bytes 393220
  7.2 321.0 %all-reduce.32.cloned.1.call-start = ((), (), s32[]{:S(2)}) async-start(), calls=%async_computation.3 | async-start | bytes 263168
  67.2 0.7 copy-start.5
  68.5 0.7 copy-start.6
  69.2 36.4 %copy-start.1 = (f32[8,64]{1,0:T(8,128)S(1)}, f32[8,64]{1,0:T(8,128)}, u32[]{:S(2)}) copy-start(f32[8,64]{1,0:T(8,128)} %param.6) | copy-start | bytes 6148
  171.5 0.5 copy-start.4
  172.1 510.4 %all-reduce.30.cloned.1.call-start = ((), (), s32[]{:S(2)}) async-start(), calls=%async_computation.2 | async-start | bytes 524288
  174.0 875.3 %all-reduce.26.cloned.1.call-start = ((), (), s32[]{:S(2)}) async-start(), calls=%async_computation | async-start | bytes 262144
  328.9 353.6 %copy-start.2 = (f32[8,64]{1,0:T(8,128)S(1)}, f32[8,64]{1,0:T(8,128)}, u32[]{:S(2)}) copy-start(f32[8,64]{1,0:T(8,128)} %param.5) | copy-start | bytes 6148
  730.5 0.7 copy-start.3
  732.9 966.4 %all-reduce.28.cloned.1.call-start = ((), (), s32[]{:S(2)}) async-start(), calls=%async_computation.1 | async-start | bytes 262144
Sparse Core Ops, SparseCore 0:
  172.2 155.9 all-reduce.31
  331.1 351.3 all-reduce.29
  733.0 316.2 all-reduce.25
  1387.1 312.2 all-reduce.27
where the time goes:
time: 1810 us
  waiting for transfers between devices  965 us (53%)
  blocking collectives  793 us (44%)
  between operations  27.5 us (2%)
    unnamed x8, waiting for transfers between devices  965 us
    unnamed x5, blocking collectives  235 us
    psum x2, blocking collectives, squared(): return lax.psum(local_inner(residual, precond), ('stu', 'que'))  193 us
    all_gather x2, blocking collectives, shards(): vt_rows = lax.all_gather(direction[0], 'que', axis=0, tiled=True)  111 us
    psum x1, blocking collectives, shards(): alpha = norm_now / lax.psum(local_inner(direction, image), ('stu', 'que'))  98.3 us
    all_gather x2, blocking collectives, shards(): va_cols = lax.all_gather(direction[1], 'stu', axis=0, tiled=True)  65.9 us
    all_gather x1, blocking collectives, shards(): theta_rows = lax.all_gather(theta, 'que', axis=0, tiled=True)  60 us
  transfers between devices with their start and end apart: 4, of which 4 were waited for; matrix products, arithmetic and copies ran while one was open for 0% of the time, Pallas kernels for 0%

commit v1 on v0

v1 whole, which is shorter than its diff:
```python
import functools

import jax
import jax.numpy as jnp
from jax import lax
from jax.experimental import pallas as pl
from jax.experimental.pallas import tpu as pltpu
from jax.sharding import PartitionSpec as P

DIMS = dict(ZL=4, X=4, ZH=2, Y=8, C=2)
K = 64
W = 128
MESH = pl.DeviceIdType.MESH
F32 = jnp.float32
HIGH = lax.Precision.HIGHEST


def dot_nn(a, b):
    return lax.dot_general(a, b, (((1,), (0,)), ((), ())), precision=HIGH, preferred_element_type=F32)


def dot_nt(a, b):
    return lax.dot_general(a, b, (((1,), (1,)), ((), ())), precision=HIGH, preferred_element_type=F32)


def dot_tn(a, b):
    return lax.dot_general(a, b, (((0,), (0,)), ((), ())), precision=HIGH, preferred_element_type=F32)


def tree_sum(parts):
    parts = list(parts)
    while len(parts) > 1:
        parts = [parts[i] + parts[i + 1] if i + 1 < len(parts) else parts[i] for i in range(0, len(parts), 2)]
    return parts[0]


def kernel(dims, names, codes_hbm, theta_ref, disc_ref, icpt_ref, out_t, out_d, out_b, codes_v, *rest):
    ZL, X, ZH, Y, C = (dims[n] for n in ("ZL", "X", "ZH", "Y", "C"))
    ref = dict(zip(names, rest))
    ssem, rsem, lsem = rest[len(names):]
    stu, que = lax.axis_index("stu"), lax.axis_index("que")
    zl, x = stu // X, stu % X
    zh, y, core = que // (Y * C), (que // C) % Y, que % C
    half = ZL // 2
    zq, zr = zl // half, zl % half
    Q = ZL * X * 8
    YB, XB = C * 8, half * 8
    SH = Y * YB
    NXY, NZC = X * Y, ZL * ZH * C

    def at(zl_, x_, zh_, y_, core_):
        return (zl_ * X + x_, (zh_ * Y + y_) * C + core_)

    def dev_y(k):
        return at(zl, x, zh, jnp.bitwise_xor(y, k), core)

    def dev_x(k):
        return at(zl, jnp.bitwise_xor(x, k), zh, y, core)

    def dev_hc(k):
        return at(zl, x, jnp.bitwise_xor(zh, k // C), y, jnp.bitwise_xor(core, k % C))

    def dev_l(k):
        return at(jnp.bitwise_xor(zl, k), x, zh, y, core)

    def dev_xy(k):
        return at(zl, jnp.bitwise_xor(x, k // Y), zh, jnp.bitwise_xor(y, k % Y), core)

    def dev_zc(k):
        return at(
            jnp.bitwise_xor(zl, k // (ZH * C)), x, jnp.bitwise_xor(zh, (k // C) % ZH), y, jnp.bitwise_xor(core, k % C)
        )

    index_of = {n: i for i, n in enumerate(names)}
    sent = []

    def send(src, name, slot, device):
        pltpu.make_async_remote_copy(
            src_ref=src,
            dst_ref=ref[name].at[slot],
            send_sem=ssem.at[index_of[name]],
            recv_sem=rsem.at[index_of[name]],
            device_id=device,
            device_id_type=MESH,
        ).start()

    def spread(name, count, dev):
        for k in range(1, count):
            send(ref[name].at[0], name, k, dev(k))
        sent.append((name, 1, count))

    def spread_loop(name, count, dev):
        def one(k, carry):
            send(ref[name].at[0], name, k, dev(k))
            return carry
        lax.fori_loop(1, count, one, 0)
        sent.append((name, 1, count))

    def scatter(src, name, count, me, dev):
        for k in range(1, count):
            send(ref[src].at[jnp.bitwise_xor(me, k)], name, k - 1, dev(k))
        sent.append((name, 0, count - 1))

    def arrived(name, lo, hi):
        r = ref[name].at[pl.ds(lo, hi - lo)]
        pltpu.make_async_copy(r, r, rsem.at[index_of[name]]).wait()

    def total(name, count):
        return tree_sum(ref[name][k] for k in range(count))

    fetch = pltpu.make_async_copy(codes_hbm, codes_v, lsem)
    fetch.start()

    barrier = pltpu.get_barrier_semaphore()

    def greet(dev):
        def one(k, carry):
            pl.semaphore_signal(barrier, inc=1, device_id=dev(k), device_id_type=MESH)
            return carry
        return one
    lax.fori_loop(1, NZC, greet(dev_zc), 0)
    lax.fori_loop(1, NXY, greet(dev_xy), 0)

    low8 = lax.broadcasted_iota(jnp.int32, (8, W), 1) // K
    th, dc = theta_ref[...], disc_ref[...]
    ref["t1"][0] = jnp.where(low8 == zh, jnp.concatenate([th, th], 1), 0.0)
    ref["d1"][0] = jnp.where(low8 == zq, jnp.concatenate([dc, dc], 1), 0.0)
    qlane = lax.broadcasted_iota(jnp.int32, (1, Q), 1)
    brow = jnp.zeros((1, Q), F32)
    for k in range(8):
        brow = jnp.where(qlane == stu * 8 + k, icpt_ref[k], brow)
    ref["b1"][0] = brow

    pl.semaphore_wait(barrier, NXY + NZC - 2)

    spread("t1", ZH * C, dev_hc)
    spread("d1", ZL, dev_l)
    spread("b1", ZL, dev_l)

    arrived("d1", 1, ZL)
    slot_l = lambda z: jnp.bitwise_xor(zl, z)
    d_own = jnp.concatenate([ref["d1"][slot_l(r)] + ref["d1"][slot_l(half + r)] for r in range(half)], 0)
    ref["d2"][0] = d_own
    spread("d2", X, dev_x)
    arrived("b1", 1, ZL)
    ref["b2"][0] = total("b1", ZL)
    spread("b2", X, dev_x)
    arrived("t1", 1, ZH * C)
    slot_hc = lambda h, c: jnp.bitwise_xor(zh, h) * C + jnp.bitwise_xor(core, c)
    t_own = jnp.concatenate([ref["t1"][slot_hc(0, c)] + ref["t1"][slot_hc(1, c)] for c in range(C)], 0)
    ref["t2"][0] = t_own
    spread("t2", Y, dev_y)

    def rows_of(name):
        return jnp.concatenate([ref[name][jnp.bitwise_xor(y, k)] for k in range(Y)], 0)

    def low(v):
        return lax.broadcasted_iota(jnp.int32, v.shape, 1) < K

    def swap(v):
        return pltpu.roll(v, K, 1)

    def cols_of(name):
        packed = jnp.concatenate(
            [ref[name][jnp.bitwise_xor(x, k), pl.ds(r * 8, 8)] for r in range(half) for k in range(X)], 0
        )
        turned = swap(packed)
        lo = low(packed)
        zero = jnp.zeros_like(packed)
        first = jnp.concatenate([jnp.where(lo, packed, zero), jnp.where(lo, turned, zero)], 0)
        second = jnp.concatenate([jnp.where(lo, zero, turned), jnp.where(lo, zero, packed)], 0)
        return first, second

    def pack_cols(v):
        upper, lower = v[: Q // 2], v[Q // 2 :]
        return jnp.where(low(upper), upper, lower)

    arrived("d2", 1, X)
    dd = cols_of("d2")
    arrived("b2", 1, X)
    bias = total("b2", X)
    fetch.wait()
    arrived("t2", 1, Y)
    theta = rows_of("t2")
    turned = swap(theta)
    lo = low(theta)
    tt = (jnp.where(lo, theta, turned), jnp.where(lo, turned, theta))

    resid, weight = [], []
    for h in range(ZH):
        prob = jax.nn.sigmoid(dot_nt(theta, dd[h]) + bias)
        code = codes_v[pl.ds(h * SH, SH)]
        observed = (code > 0).astype(F32)
        correct = (code == 2).astype(F32)
        resid.append(observed * (prob - correct))
        weight.append(observed * prob * (1.0 - prob))

    def row_part(u, d):
        return dot_nn(u[0], d[0]) + dot_nn(u[1], d[1])

    def col_part(u, t):
        return pack_cols(dot_tn(u[0], t[0]) + dot_tn(u[1], t[1]))

    def col_sum(u):
        return jnp.sum(u[0], 0, keepdims=True) + jnp.sum(u[1], 0, keepdims=True)

    def put_rows(name, offset, v):
        for k in range(Y):
            ref[name][k, pl.ds(offset, YB)] = v[k * YB : (k + 1) * YB]

    def put_cols(name, offset, v):
        for k in range(X):
            for r in range(half):
                start = (r * X + k) * 8
                ref[name][k, pl.ds(offset + r * 8, 8)] = v[start : start + 8]

    def reduce_all(tag, row_list, col_list, sums, during_first=None, during_second=None):
        for i, v in enumerate(row_list):
            put_rows("ra" + tag, i * YB, v)
        scatter("ra" + tag, "rb" + tag, Y, y, dev_y)
        for i, v in enumerate(col_list):
            put_cols("ca" + tag, i * XB, v)
        scatter("ca" + tag, "cb" + tag, X, x, dev_x)
        ref["sa" + tag][0] = sums
        spread("sa" + tag, X, dev_x)
        if during_first is not None:
            during_first()
        arrived("cb" + tag, 0, X - 1)
        ref["cc" + tag][0] = tree_sum([ref["ca" + tag][x]] + [ref["cb" + tag][k] for k in range(X - 1)])
        spread("cc" + tag, ZL, dev_l)
        arrived("sa" + tag, 1, X)
        ref["sb" + tag][0] = total("sa" + tag, X)
        spread("sb" + tag, ZL, dev_l)
        arrived("rb" + tag, 0, Y - 1)
        ref["rc" + tag][0] = tree_sum([ref["ra" + tag][y]] + [ref["rb" + tag][k] for k in range(Y - 1)])
        spread("rc" + tag, ZH * C, dev_hc)
        if during_second is not None:
            during_second()
        arrived("cc" + tag, 1, ZL)
        cols = total("cc" + tag, ZL)
        arrived("sb" + tag, 1, ZL)
        sums = total("sb" + tag, ZL)
        arrived("rc" + tag, 1, ZH * C)
        rows = total("rc" + tag, ZH * C)
        return rows, cols, sums

    def gather_start(tag, rows, cols):
        ref["rg" + tag][0] = rows
        spread("rg" + tag, Y, dev_y)
        ref["cg" + tag][0] = cols
        spread("cg" + tag, X, dev_x)

    def change_of(tag, vb):
        arrived("cg" + tag, 1, X)
        va = cols_of("cg" + tag)
        arrived("rg" + tag, 1, Y)
        left = jnp.concatenate([rows_of("rg" + tag), theta], 1)
        return [dot_nt(left, jnp.concatenate([dd[h], va[h]], 1)) + vb for h in range(ZH)]

    def lanes(v):
        s = jnp.sum(v, 0, keepdims=True)
        if s.shape[1] < W:
            s = jnp.concatenate([s, jnp.zeros((1, W - s.shape[1]), F32)], 1)
        return s

    def inner(u, v):
        rows = lanes(u[0] * v[0]) * (1.0 / (ZH * C))
        cols = lanes(u[1] * v[1]) * (1.0 / ZL)
        return rows + cols + lanes(u[2] * v[2]) * (1.0 / (ZL * X))

    def first_round(tag, values):
        for i, v in enumerate(values):
            ref["p" + tag][0, pl.ds(i, 1)] = v
        spread_loop("p" + tag, NXY, dev_xy)

    def second_round(tag):
        arrived("p" + tag, 1, NXY)
        ref["q" + tag][0] = jnp.sum(ref["p" + tag][...], 0)
        spread_loop("q" + tag, NZC, dev_zc)

    def last_round(tag):
        arrived("q" + tag, 1, NZC)
        return jnp.sum(jnp.sum(ref["q" + tag][...], 0), 1, keepdims=True)

    d2 = [d * d for d in dd]
    t2 = [t * t for t in tt]
    sums = jnp.concatenate([col_sum(resid), col_sum(weight)], 0)
    rows, cols, sums = reduce_all(
        "1",
        (row_part(resid, dd), row_part(weight, d2)),
        (col_part(resid, tt), col_part(weight, t2)),
        sums,
    )
    r = (-(rows[:YB] + t_own), -(cols[:XB] + d_own), -(sums[0:1] + bias))
    dg = (rows[YB:] + 1.0, cols[XB:] + 1.0, sums[1:2] + 1.0)
    z = [a / b for a, b in zip(r, dg)]
    gather_start("1", z[0], z[1])
    rz_part = inner(r, z)
    zz_part = inner(z, z)
    change = change_of("1", z[2])
    scaled = [w * c for w, c in zip(weight, change)]
    pq_part = lanes(scaled[0] * change[0]) + lanes(scaled[1] * change[1]) + zz_part

    rows, cols, sums = reduce_all(
        "2",
        (row_part(scaled, dd),),
        (col_part(scaled, tt),),
        col_sum(scaled),
        during_first=lambda: first_round("1", (rz_part, pq_part)),
        during_second=lambda: second_round("1"),
    )
    image = (rows + z[0], cols + z[1], sums + z[2])
    scalars = last_round("1")
    rz, pq = scalars[0:1], scalars[1:2]
    alpha = rz / pq
    r = [a - alpha * b for a, b in zip(r, image)]
    z_next = [a / b for a, b in zip(r, dg)]
    gather_start("2", z_next[0], z_next[1])
    first_round("2", (inner(r, z_next),))
    change_next = change_of("2", z_next[2])
    second_round("2")
    new = last_round("2")
    beta = new / rz
    p = [a + beta * b for a, b in zip(z_next, z)]
    change = [a + beta * b for a, b in zip(change_next, change)]
    curv = inner(p, p)
    for w, c in zip(weight, change):
        curv = curv + lanes(w * c * c)
    first_round("3", (curv,))
    second_round("3")
    alpha_two = new / last_round("3")
    step = [(alpha * a + alpha_two * b) * jnp.sqrt(d) for a, b, d in zip(z, p, dg)]

    ref["xt"][...] = step[0]
    mine = ref["xt"][pl.ds(pl.multiple_of(core * 8, 8), 8)]
    out_t[...] = jnp.where(zh == 0, mine, swap(mine))[:, :K]
    ref["xd"][...] = step[1]
    mine = ref["xd"][pl.ds(pl.multiple_of(zr * 8, 8), 8)]
    out_d[...] = jnp.where(zq == 0, mine, swap(mine))[:, :K]
    out_b[...] = pltpu.roll(step[2], lax.rem(Q - stu * 8, Q), 1)[:, :8]

    for name, first, last in sent:
        like = ref[name].at[pl.ds(first, last - first)]
        pltpu.make_async_copy(like, like, ssem.at[index_of[name]]).wait()


def buffers(dims):
    ZL, X, ZH, Y, C = (dims[n] for n in ("ZL", "X", "ZH", "Y", "C"))
    Q, YB, XB = ZL * X * 8, C * 8, ZL // 2 * 8
    shapes = {
        "t1": (ZH * C, 8, W), "d1": (ZL, 8, W), "b1": (ZL, 1, Q),
        "t2": (Y, YB, W), "d2": (X, XB, W), "b2": (X, 1, Q),
    }
    for tag, n in (("1", 2), ("2", 1)):
        shapes["ra" + tag] = (Y, n * YB, W)
        shapes["rb" + tag] = (Y - 1, n * YB, W)
        shapes["rc" + tag] = (ZH * C, n * YB, W)
        shapes["ca" + tag] = (X, n * XB, W)
        shapes["cb" + tag] = (X - 1, n * XB, W)
        shapes["cc" + tag] = (ZL, n * XB, W)
        shapes["sa" + tag] = (X, n, Q)
        shapes["sb" + tag] = (ZL, n, Q)
        shapes["rg" + tag] = (Y, YB, W)
        shapes["cg" + tag] = (X, XB, W)
    for tag, n in (("1", 2), ("2", 1), ("3", 1)):
        shapes["p" + tag] = (X * Y, n, W)
        shapes["q" + tag] = (ZL * ZH * C, n, W)
    shapes["xt"] = (YB, W)
    shapes["xd"] = (XB, W)
    return shapes


def shards(dims, codes, theta, disc, intercept):
    shapes = buffers(dims)
    names = tuple(shapes)
    vmem = pl.BlockSpec(memory_space=pltpu.VMEM)
    outs = pl.pallas_call(
        functools.partial(kernel, dims, names),
        out_shape=(
            jax.ShapeDtypeStruct(theta.shape, F32),
            jax.ShapeDtypeStruct(disc.shape, F32),
            jax.ShapeDtypeStruct((1, intercept.shape[0]), F32),
        ),
        in_specs=[pl.BlockSpec(memory_space=pl.ANY), vmem, vmem, pl.BlockSpec(memory_space=pltpu.SMEM)],
        out_specs=(vmem, vmem, vmem),
        scratch_shapes=[pltpu.VMEM(codes.shape, jnp.int32)]
        + [pltpu.VMEM(shape, F32) for shape in shapes.values()]
        + [
            pltpu.SemaphoreType.DMA((len(names),)),
            pltpu.SemaphoreType.DMA((len(names),)),
            pltpu.SemaphoreType.DMA,
        ],
        compiler_params=pltpu.CompilerParams(collective_id=0, has_side_effects=True),
    )(codes, theta, disc, intercept)
    return outs[0], outs[1], outs[2].reshape(intercept.shape)


def solution(mesh):
    return jax.shard_map(
        functools.partial(shards, DIMS),
        mesh=mesh,
        in_specs=(P("stu", "que"), P(("stu", "que"), None), P(("que", "stu"), None), P(("que", "stu"))),
        out_specs=(P(("stu", "que"), None), P(("que", "stu"), None), P(("que", "stu"))),
        check_vma=False,
    )
```

time: 1810 us -> 83.3 us (0.05)
  waiting for transfers between devices: 965 us -> 0 us
  blocking collectives: 793 us -> 0 us
  Pallas kernels: 0 us -> 80 us
  between operations: 27.5 us -> 0.65 us
    unnamed x8 -> x0, waiting for transfers between devices: 965 us -> none
    psum x3 -> x0, blocking collectives: 291 us -> none  [the longest x2 193 us: squared(): return lax.psum(local_inner(residual, precond), ('stu', 'que'))]
    all_gather x6 -> x0, blocking collectives: 267 us -> none  [the longest x2 111 us: shards(): vt_rows = lax.all_gather(direction[0], 'que', axis=0, tiled=True)]
    unnamed x5 -> x0, blocking collectives: 235 us -> none
    pallas_call x0 -> x1, Pallas kernels: none -> 80 us  [shards(): pl.pallas_call(functools.partial(kernel, dims, names), out_shape=(jax.Sha...]
  transfers between devices with their start and end apart: 4 -> 0, of which waited for: 4 -> 0; matrix products, arithmetic and copies ran while one was open for 0% -> 0% of each run, Pallas kernels for 0% -> 0%
where the time goes in v1:
time: 83.3 us; the launch traced here: 83.1 us
  Pallas kernels  80 us (96%)
  local copies, waits for them, and re-layouts  2.45 us (3%)
    pallas_call x1, Pallas kernels, shards(): pl.pallas_call(functools.partial(kernel, dims, names), out_shape=(jax.Sha...  80 us
    unnamed x9, local copies, waits for them, and re-layouts  2.45 us

profile of v1, /device:TPU:1, one launch (start us, length us, event | category | flops | bytes accessed | tf_op | source)
XLA Modules:
  0.0 83.1 jit_solution(11279699916361363496)
XLA Ops:
  0.6 80.0 %shard_map.67 = (f32[8,64]{1,0:T(8,128)}, f32[8,64]{1,0:T(8,128)}, f32[1,8]{1,0:T(1,128)}) custom-call(s32[256,128]{1,0:T(8,128)} %codes_hbm.1, f32[8,64]{1,0:T(8,128)} %theta_ref.1, f32[8,64]{1,0:T(8,128)} %disc_ref.1, f32[8]{0:T(128)} %icpt_ref.1), custom_call_target="tpu_custom_call" | custom-call | tf_op jit(solution)/shard_map/pallas_call | solution.py:377
  80.6 0.0 copy-start.1
  80.6 0.7 copy-done.1
  81.3 0.0 copy-start
  81.3 0.6 copy.10
  81.9 0.1 copy-done
  82.0 0.0 copy-start.2
  82.0 0.6 copy.11
  82.6 0.0 copy-done.2
  82.6 0.5 copy.12
Async XLA Ops:
  80.6 0.7 copy-start.1
  81.3 0.7 copy-start
  82.0 0.6 copy-start.2

commit v2 on v1

--- a/solution.py
+++ b/solution.py
@@ -34,10 +34,14 @@
     return parts[0]
 
 
-def kernel(dims, names, codes_hbm, theta_ref, disc_ref, icpt_ref, out_t, out_d, out_b, codes_v, *rest):
+def far_first(count):
+    return sorted(range(1, count), key=lambda k: ({4: 0, 5: 1, 3: 2, 7: 3, 6: 4, 2: 5, 1: 6}.get(k % 8, 7), -k))
+
+
+def kernel(dims, names, codes_hbm, theta_hbm, disc_hbm, icpt_hbm, out_t, out_d, out_b, *rest):
     ZL, X, ZH, Y, C = (dims[n] for n in ("ZL", "X", "ZH", "Y", "C"))
     ref = dict(zip(names, rest))
-    ssem, rsem, lsem = rest[len(names):]
+    codes_v, theta_v, disc_v, icpt_s, made_t, made_d, made_b, ssem, rsem, lsem = rest[len(names):]
     stu, que = lax.axis_index("stu"), lax.axis_index("que")
     zl, x = stu // X, stu % X
     zh, y, core = que // (Y * C), (que // C) % Y, que % C
@@ -85,19 +89,12 @@
         ).start()
 
     def spread(name, count, dev):
-        for k in range(1, count):
+        for k in far_first(count):
             send(ref[name].at[0], name, k, dev(k))
         sent.append((name, 1, count))
 
-    def spread_loop(name, count, dev):
-        def one(k, carry):
-            send(ref[name].at[0], name, k, dev(k))
-            return carry
-        lax.fori_loop(1, count, one, 0)
-        sent.append((name, 1, count))
-
     def scatter(src, name, count, me, dev):
-        for k in range(1, count):
+        for k in far_first(count):
             send(ref[src].at[jnp.bitwise_xor(me, k)], name, k - 1, dev(k))
         sent.append((name, 0, count - 1))
 
@@ -108,30 +105,37 @@
     def total(name, count):
         return tree_sum(ref[name][k] for k in range(count))
 
-    fetch = pltpu.make_async_copy(codes_hbm, codes_v, lsem)
-    fetch.start()
+    fetches = [
+        pltpu.make_async_copy(src, dst, lsem.at[i])
+        for i, (src, dst) in enumerate(
+            ((theta_hbm, theta_v), (disc_hbm, disc_v), (icpt_hbm, icpt_s), (codes_hbm, codes_v))
+        )
+    ]
+    for fetch in fetches[:3]:
+        fetch.start()
 
     barrier = pltpu.get_barrier_semaphore()
-
-    def greet(dev):
-        def one(k, carry):
-            pl.semaphore_signal(barrier, inc=1, device_id=dev(k), device_id_type=MESH)
-            return carry
-        return one
-    lax.fori_loop(1, NZC, greet(dev_zc), 0)
-    lax.fori_loop(1, NXY, greet(dev_xy), 0)
+    partners = [dev_y(k) for k in far_first(Y)] + [dev_hc(k) for k in far_first(ZH * C)]
+    partners += [dev_l(k) for k in far_first(ZL)] + [dev_x(k) for k in far_first(X)]
+    for partner in partners:
+        pl.semaphore_signal(barrier, inc=1, device_id=partner, device_id_type=MESH)
+    fetches[3].start()
 
     low8 = lax.broadcasted_iota(jnp.int32, (8, W), 1) // K
-    th, dc = theta_ref[...], disc_ref[...]
+    fetches[0].wait()
+    th = theta_v[...]
     ref["t1"][0] = jnp.where(low8 == zh, jnp.concatenate([th, th], 1), 0.0)
+    fetches[1].wait()
+    dc = disc_v[...]
     ref["d1"][0] = jnp.where(low8 == zq, jnp.concatenate([dc, dc], 1), 0.0)
+    fetches[2].wait()
     qlane = lax.broadcasted_iota(jnp.int32, (1, Q), 1)
     brow = jnp.zeros((1, Q), F32)
     for k in range(8):
-        brow = jnp.where(qlane == stu * 8 + k, icpt_ref[k], brow)
+        brow = jnp.where(qlane == stu * 8 + k, icpt_s[k], brow)
     ref["b1"][0] = brow
 
-    pl.semaphore_wait(barrier, NXY + NZC - 2)
+    pl.semaphore_wait(barrier, len(partners))
 
     spread("t1", ZH * C, dev_hc)
     spread("d1", ZL, dev_l)
@@ -179,7 +183,7 @@
     dd = cols_of("d2")
     arrived("b2", 1, X)
     bias = total("b2", X)
-    fetch.wait()
+    fetches[3].wait()
     arrived("t2", 1, Y)
     theta = rows_of("t2")
     turned = swap(theta)
@@ -214,7 +218,7 @@
                 start = (r * X + k) * 8
                 ref[name][k, pl.ds(offset + r * 8, 8)] = v[start : start + 8]
 
-    def reduce_all(tag, row_list, col_list, sums, during_first=None, during_second=None):
+    def reduce_all(tag, row_list, col_list, sums, between=None):
         for i, v in enumerate(row_list):
             put_rows("ra" + tag, i * YB, v)
         scatter("ra" + tag, "rb" + tag, Y, y, dev_y)
@@ -223,19 +227,17 @@
         scatter("ca" + tag, "cb" + tag, X, x, dev_x)
         ref["sa" + tag][0] = sums
         spread("sa" + tag, X, dev_x)
-        if during_first is not None:
-            during_first()
         arrived("cb" + tag, 0, X - 1)
         ref["cc" + tag][0] = tree_sum([ref["ca" + tag][x]] + [ref["cb" + tag][k] for k in range(X - 1)])
         spread("cc" + tag, ZL, dev_l)
         arrived("sa" + tag, 1, X)
         ref["sb" + tag][0] = total("sa" + tag, X)
         spread("sb" + tag, ZL, dev_l)
+        if between is not None:
+            between()
         arrived("rb" + tag, 0, Y - 1)
         ref["rc" + tag][0] = tree_sum([ref["ra" + tag][y]] + [ref["rb" + tag][k] for k in range(Y - 1)])
         spread("rc" + tag, ZH * C, dev_hc)
-        if during_second is not None:
-            during_second()
         arrived("cc" + tag, 1, ZL)
         cols = total("cc" + tag, ZL)
         arrived("sb" + tag, 1, ZL)
@@ -271,12 +273,12 @@
     def first_round(tag, values):
         for i, v in enumerate(values):
             ref["p" + tag][0, pl.ds(i, 1)] = v
-        spread_loop("p" + tag, NXY, dev_xy)
+        spread("p" + tag, NXY, dev_xy)
 
     def second_round(tag):
         arrived("p" + tag, 1, NXY)
         ref["q" + tag][0] = jnp.sum(ref["p" + tag][...], 0)
-        spread_loop("q" + tag, NZC, dev_zc)
+        spread("q" + tag, NZC, dev_zc)
 
     def last_round(tag):
         arrived("q" + tag, 1, NZC)
@@ -300,14 +302,13 @@
     change = change_of("1", z[2])
     scaled = [w * c for w, c in zip(weight, change)]
     pq_part = lanes(scaled[0] * change[0]) + lanes(scaled[1] * change[1]) + zz_part
-
+    first_round("1", (rz_part, pq_part))
     rows, cols, sums = reduce_all(
         "2",
         (row_part(scaled, dd),),
         (col_part(scaled, tt),),
         col_sum(scaled),
-        during_first=lambda: first_round("1", (rz_part, pq_part)),
-        during_second=lambda: second_round("1"),
+        between=lambda: second_round("1"),
     )
     image = (rows + z[0], cols + z[1], sums + z[2])
     scalars = last_round("1")
@@ -316,32 +317,55 @@
     r = [a - alpha * b for a, b in zip(r, image)]
     z_next = [a / b for a, b in zip(r, dg)]
     gather_start("2", z_next[0], z_next[1])
-    first_round("2", (inner(r, z_next),))
+    new_part = inner(r, z_next)
+    own_part, cross_part = inner(z_next, z_next), inner(z_next, z)
     change_next = change_of("2", z_next[2])
+    for w, c, n in zip(weight, change, change_next):
+        wn = w * n
+        own_part = own_part + lanes(wn * n)
+        cross_part = cross_part + lanes(wn * c)
+    first_round("2", (new_part, own_part, cross_part))
     second_round("2")
-    new = last_round("2")
+    scalars = last_round("2")
+    new, own, cross = scalars[0:1], scalars[1:2], scalars[2:3]
     beta = new / rz
-    p = [a + beta * b for a, b in zip(z_next, z)]
-    change = [a + beta * b for a, b in zip(change_next, change)]
-    curv = inner(p, p)
-    for w, c in zip(weight, change):
-        curv = curv + lanes(w * c * c)
-    first_round("3", (curv,))
-    second_round("3")
-    alpha_two = new / last_round("3")
-    step = [(alpha * a + alpha_two * b) * jnp.sqrt(d) for a, b, d in zip(z, p, dg)]
+    alpha_two = new / (own + 2.0 * beta * cross + beta * beta * pq)
+    step = [
+        (alpha * a + alpha_two * (b + beta * a)) * jnp.sqrt(d) for a, b, d in zip(z, z_next, dg)
+    ]
 
     ref["xt"][...] = step[0]
     mine = ref["xt"][pl.ds(pl.multiple_of(core * 8, 8), 8)]
-    out_t[...] = jnp.where(zh == 0, mine, swap(mine))[:, :K]
+    made_t[...] = jnp.where(zh == 0, mine, swap(mine))[:, :K]
     ref["xd"][...] = step[1]
     mine = ref["xd"][pl.ds(pl.multiple_of(zr * 8, 8), 8)]
-    out_d[...] = jnp.where(zq == 0, mine, swap(mine))[:, :K]
-    out_b[...] = pltpu.roll(step[2], lax.rem(Q - stu * 8, Q), 1)[:, :8]
+    made_d[...] = jnp.where(zq == 0, mine, swap(mine))[:, :K]
+    made_b[...] = pltpu.roll(step[2], lax.rem(Q - stu * 8, Q), 1)[:, :8]
+    stores = [
+        pltpu.make_async_copy(src, dst, lsem.at[4 + i])
+        for i, (src, dst) in enumerate(((made_t, out_t), (made_d, out_d), (made_b, out_b)))
+    ]
+    for store in stores:
+        store.start()
 
     for name, first, last in sent:
         like = ref[name].at[pl.ds(first, last - first)]
         pltpu.make_async_copy(like, like, ssem.at[index_of[name]]).wait()
+    for store in stores:
+        store.wait()
+
+
+def hand_over(*refs):
+    ins, outs, held, sems = refs[:3], refs[3:6], refs[6:9], refs[9]
+    first = [pltpu.make_async_copy(a, b, sems.at[i]) for i, (a, b) in enumerate(zip(ins, held))]
+    second = [pltpu.make_async_copy(a, b, sems.at[3 + i]) for i, (a, b) in enumerate(zip(held, outs))]
+    for copy in first:
+        copy.start()
+    for a, b in zip(first, second):
+        a.wait()
+        b.start()
+    for copy in second:
+        copy.wait()
 
 
 def buffers(dims):
@@ -362,7 +386,7 @@
         shapes["sb" + tag] = (ZL, n, Q)
         shapes["rg" + tag] = (Y, YB, W)
         shapes["cg" + tag] = (X, XB, W)
-    for tag, n in (("1", 2), ("2", 1), ("3", 1)):
+    for tag, n in (("1", 2), ("2", 3)):
         shapes["p" + tag] = (X * Y, n, W)
         shapes["q" + tag] = (ZL * ZH * C, n, W)
     shapes["xt"] = (YB, W)
@@ -373,25 +397,39 @@
 def shards(dims, codes, theta, disc, intercept):
     shapes = buffers(dims)
     names = tuple(shapes)
-    vmem = pl.BlockSpec(memory_space=pltpu.VMEM)
+    made = (
+        jax.ShapeDtypeStruct(theta.shape, F32),
+        jax.ShapeDtypeStruct(disc.shape, F32),
+        jax.ShapeDtypeStruct((1, intercept.shape[0]), F32),
+    )
+    hbm = pl.BlockSpec(memory_space=pltpu.HBM)
     outs = pl.pallas_call(
         functools.partial(kernel, dims, names),
-        out_shape=(
-            jax.ShapeDtypeStruct(theta.shape, F32),
-            jax.ShapeDtypeStruct(disc.shape, F32),
-            jax.ShapeDtypeStruct((1, intercept.shape[0]), F32),
-        ),
-        in_specs=[pl.BlockSpec(memory_space=pl.ANY), vmem, vmem, pl.BlockSpec(memory_space=pltpu.SMEM)],
-        out_specs=(vmem, vmem, vmem),
-        scratch_shapes=[pltpu.VMEM(codes.shape, jnp.int32)]
-        + [pltpu.VMEM(shape, F32) for shape in shapes.values()]
+        out_shape=made,
+        in_specs=[hbm, hbm, hbm, hbm],
+        out_specs=(hbm, hbm, hbm),
+        scratch_shapes=[pltpu.VMEM(shape, F32) for shape in shapes.values()]
+        + [
+            pltpu.VMEM(codes.shape, jnp.int32),
+            pltpu.VMEM(theta.shape, F32),
+            pltpu.VMEM(disc.shape, F32),
+            pltpu.SMEM(intercept.shape, F32),
+        ]
+        + [pltpu.VMEM(s.shape, F32) for s in made]
         + [
             pltpu.SemaphoreType.DMA((len(names),)),
             pltpu.SemaphoreType.DMA((len(names),)),
-            pltpu.SemaphoreType.DMA,
+            pltpu.SemaphoreType.DMA((7,)),
         ],
         compiler_params=pltpu.CompilerParams(collective_id=0, has_side_effects=True),
     )(codes, theta, disc, intercept)
+    outs = pl.pallas_call(
+        hand_over,
+        out_shape=made,
+        in_specs=[hbm, hbm, hbm],
+        out_specs=(hbm, hbm, hbm),
+        scratch_shapes=[pltpu.VMEM(s.shape, F32) for s in made] + [pltpu.SemaphoreType.DMA((6,))],
+    )(*outs)
     return outs[0], outs[1], outs[2].reshape(intercept.shape)
 
 

time: 83.3 us -> 69.8 us (0.84)
  Pallas kernels: 80 us -> 69 us
  local copies, waits for them, and re-layouts: 2.45 us -> 0 us
    pallas_call x1 -> x2, Pallas kernels: 80 us -> 69 us  [the longest x1 67.6 us: shards(): pl.pallas_call(functools.partial(kernel, dims, names), out_shape=made, in...]
    unnamed x9 -> x0, local copies, waits for them, and re-layouts: 2.45 us -> none
where the time goes in v2:
time: 69.8 us; the launch traced here: 69.6 us
  Pallas kernels  69 us (99%)
    pallas_call x1, Pallas kernels, shards(): pl.pallas_call(functools.partial(kernel, dims, names), out_shape=made, in...  67.6 us

profile of v2, /device:TPU:1, one launch (start us, length us, event | category | flops | bytes accessed | tf_op | source)
XLA Modules:
  0.0 69.6 jit_solution(18060105938811046965)
XLA Ops:
  0.6 67.6 %shard_map.67 = (f32[8,64]{1,0:T(8,128)}, f32[8,64]{1,0:T(8,128)}, f32[1,8]{1,0:T(1,128)}) custom-call(s32[256,128]{1,0:T(8,128)} %codes_hbm.1, f32[8,64]{1,0:T(8,128)} %theta_hbm.1, f32[8,64]{1,0:T(8,128)} %disc_hbm.1, f32[8]{0:T(128)} %icpt_hbm.1), custom_call_target="tpu_custom_call" | custom-call | tf_op jit(solution)/shard_map/pallas_call | solution.py:406
  68.3 1.3 %shard_map.68 = (f32[8,64]{1,0:T(8,128)}, f32[8,64]{1,0:T(8,128)}, f32[1,8]{1,0:T(1,128)}) custom-call(f32[8,64]{1,0:T(8,128)} %get-tuple-element.9.refs_0_, f32[8,64]{1,0:T(8,128)} %get-tuple-element.10.refs_1_, f32[1,8]{1,0:T(1,128)} %get-tuple-element.11.refs_2_), custom_call_target="tpu_custom_call" | custom-call | tf_op jit(solution)/shard_map/pallas_call | solution.py:426

commit v3 on v2

--- a/solution.py
+++ b/solution.py
@@ -12,19 +12,33 @@
 W = 128
 MESH = pl.DeviceIdType.MESH
 F32 = jnp.float32
-HIGH = lax.Precision.HIGHEST
+
+
+def split(v):
+    head = v.astype(jnp.bfloat16)
+    return head, (v - head.astype(F32)).astype(jnp.bfloat16)
+
+
+def dot(a, b, ca, cb):
+    def one(u, v):
+        return lax.dot_general(u, v, (((ca,), (cb,)), ((), ())), preferred_element_type=F32)
+    return one(a[0], b[0]) + (one(a[0], b[1]) + one(a[1], b[0]))
 
 
 def dot_nn(a, b):
-    return lax.dot_general(a, b, (((1,), (0,)), ((), ())), precision=HIGH, preferred_element_type=F32)
+    return dot(a, b, 1, 0)
 
 
 def dot_nt(a, b):
-    return lax.dot_general(a, b, (((1,), (1,)), ((), ())), precision=HIGH, preferred_element_type=F32)
+    return dot(a, b, 1, 1)
 
 
 def dot_tn(a, b):
-    return lax.dot_general(a, b, (((0,), (0,)), ((), ())), precision=HIGH, preferred_element_type=F32)
+    return dot(a, b, 0, 0)
+
+
+def beside(a, b):
+    return tuple(jnp.concatenate([u, v], 1) for u, v in zip(a, b))
 
 
 def tree_sum(parts):
@@ -41,7 +55,7 @@
 def kernel(dims, names, codes_hbm, theta_hbm, disc_hbm, icpt_hbm, out_t, out_d, out_b, *rest):
     ZL, X, ZH, Y, C = (dims[n] for n in ("ZL", "X", "ZH", "Y", "C"))
     ref = dict(zip(names, rest))
-    codes_v, theta_v, disc_v, icpt_s, made_t, made_d, made_b, ssem, rsem, lsem = rest[len(names):]
+    codes_v, theta_v, disc_v, icpt_s, ssem, rsem, lsem = rest[len(names):]
     stu, que = lax.axis_index("stu"), lax.axis_index("que")
     zl, x = stu // X, stu % X
     zh, y, core = que // (Y * C), (que // C) % Y, que % C
@@ -190,9 +204,11 @@
     lo = low(theta)
     tt = (jnp.where(lo, theta, turned), jnp.where(lo, turned, theta))
 
+    theta_s, dd_s, tt_s = split(theta), [split(d) for d in dd], [split(t) for t in tt]
+
     resid, weight = [], []
     for h in range(ZH):
-        prob = jax.nn.sigmoid(dot_nt(theta, dd[h]) + bias)
+        prob = jax.nn.sigmoid(dot_nt(theta_s, dd_s[h]) + bias)
         code = codes_v[pl.ds(h * SH, SH)]
         observed = (code > 0).astype(F32)
         correct = (code == 2).astype(F32)
@@ -233,11 +249,11 @@
         arrived("sa" + tag, 1, X)
         ref["sb" + tag][0] = total("sa" + tag, X)
         spread("sb" + tag, ZL, dev_l)
-        if between is not None:
-            between()
         arrived("rb" + tag, 0, Y - 1)
         ref["rc" + tag][0] = tree_sum([ref["ra" + tag][y]] + [ref["rb" + tag][k] for k in range(Y - 1)])
         spread("rc" + tag, ZH * C, dev_hc)
+        if between is not None:
+            between()
         arrived("cc" + tag, 1, ZL)
         cols = total("cc" + tag, ZL)
         arrived("sb" + tag, 1, ZL)
@@ -256,8 +272,8 @@
         arrived("cg" + tag, 1, X)
         va = cols_of("cg" + tag)
         arrived("rg" + tag, 1, Y)
-        left = jnp.concatenate([rows_of("rg" + tag), theta], 1)
-        return [dot_nt(left, jnp.concatenate([dd[h], va[h]], 1)) + vb for h in range(ZH)]
+        left = beside(split(rows_of("rg" + tag)), theta_s)
+        return [dot_nt(left, beside(dd_s[h], split(va[h]))) + vb for h in range(ZH)]
 
     def lanes(v):
         s = jnp.sum(v, 0, keepdims=True)
@@ -284,13 +300,14 @@
         arrived("q" + tag, 1, NZC)
         return jnp.sum(jnp.sum(ref["q" + tag][...], 0), 1, keepdims=True)
 
-    d2 = [d * d for d in dd]
-    t2 = [t * t for t in tt]
+    d2 = [split(d * d) for d in dd]
+    t2 = [split(t * t) for t in tt]
+    resid_s, weight_s = [split(u) for u in resid], [split(u) for u in weight]
     sums = jnp.concatenate([col_sum(resid), col_sum(weight)], 0)
     rows, cols, sums = reduce_all(
         "1",
-        (row_part(resid, dd), row_part(weight, d2)),
-        (col_part(resid, tt), col_part(weight, t2)),
+        (row_part(resid_s, dd_s), row_part(weight_s, d2)),
+        (col_part(resid_s, tt_s), col_part(weight_s, t2)),
         sums,
     )
     r = (-(rows[:YB] + t_own), -(cols[:XB] + d_own), -(sums[0:1] + bias))
@@ -301,26 +318,28 @@
     zz_part = inner(z, z)
     change = change_of("1", z[2])
     scaled = [w * c for w, c in zip(weight, change)]
+    scaled_s = [split(u) for u in scaled]
     pq_part = lanes(scaled[0] * change[0]) + lanes(scaled[1] * change[1]) + zz_part
     first_round("1", (rz_part, pq_part))
     rows, cols, sums = reduce_all(
         "2",
-        (row_part(scaled, dd),),
-        (col_part(scaled, tt),),
+        (row_part(scaled_s, dd_s),),
+        (col_part(scaled_s, tt_s),),
         col_sum(scaled),
         between=lambda: second_round("1"),
     )
     image = (rows + z[0], cols + z[1], sums + z[2])
+    scaled_image = [a / b for a, b in zip(image, dg)]
+    gather_start("2", scaled_image[0], scaled_image[1])
     scalars = last_round("1")
     rz, pq = scalars[0:1], scalars[1:2]
     alpha = rz / pq
     r = [a - alpha * b for a, b in zip(r, image)]
     z_next = [a / b for a, b in zip(r, dg)]
-    gather_start("2", z_next[0], z_next[1])
     new_part = inner(r, z_next)
     own_part, cross_part = inner(z_next, z_next), inner(z_next, z)
-    change_next = change_of("2", z_next[2])
-    for w, c, n in zip(weight, change, change_next):
+    for w, c, s in zip(weight, change, change_of("2", scaled_image[2])):
+        n = c - alpha * s
         wn = w * n
         own_part = own_part + lanes(wn * n)
         cross_part = cross_part + lanes(wn * c)
@@ -336,35 +355,23 @@
 
     ref["xt"][...] = step[0]
     mine = ref["xt"][pl.ds(pl.multiple_of(core * 8, 8), 8)]
-    made_t[...] = jnp.where(zh == 0, mine, swap(mine))[:, :K]
+    out_t[...] = jnp.where(zh == 0, mine, swap(mine))[:, :K]
     ref["xd"][...] = step[1]
     mine = ref["xd"][pl.ds(pl.multiple_of(zr * 8, 8), 8)]
-    made_d[...] = jnp.where(zq == 0, mine, swap(mine))[:, :K]
-    made_b[...] = pltpu.roll(step[2], lax.rem(Q - stu * 8, Q), 1)[:, :8]
-    stores = [
-        pltpu.make_async_copy(src, dst, lsem.at[4 + i])
-        for i, (src, dst) in enumerate(((made_t, out_t), (made_d, out_d), (made_b, out_b)))
-    ]
-    for store in stores:
-        store.start()
+    out_d[...] = jnp.where(zq == 0, mine, swap(mine))[:, :K]
+    out_b[...] = pltpu.roll(step[2], lax.rem(Q - stu * 8, Q), 1)[:, :8]
 
     for name, first, last in sent:
         like = ref[name].at[pl.ds(first, last - first)]
         pltpu.make_async_copy(like, like, ssem.at[index_of[name]]).wait()
-    for store in stores:
-        store.wait()
 
 
 def hand_over(*refs):
-    ins, outs, held, sems = refs[:3], refs[3:6], refs[6:9], refs[9]
-    first = [pltpu.make_async_copy(a, b, sems.at[i]) for i, (a, b) in enumerate(zip(ins, held))]
-    second = [pltpu.make_async_copy(a, b, sems.at[3 + i]) for i, (a, b) in enumerate(zip(held, outs))]
-    for copy in first:
+    ins, outs, sems = refs[:3], refs[3:6], refs[6]
+    copies = [pltpu.make_async_copy(a, b, sems.at[i]) for i, (a, b) in enumerate(zip(ins, outs))]
+    for copy in copies:
         copy.start()
-    for a, b in zip(first, second):
-        a.wait()
-        b.start()
-    for copy in second:
+    for copy in copies:
         copy.wait()
 
 
@@ -402,33 +409,31 @@
         jax.ShapeDtypeStruct(disc.shape, F32),
         jax.ShapeDtypeStruct((1, intercept.shape[0]), F32),
     )
-    hbm = pl.BlockSpec(memory_space=pltpu.HBM)
+    hbm, vmem = pl.BlockSpec(memory_space=pltpu.HBM), pl.BlockSpec(memory_space=pltpu.VMEM)
     outs = pl.pallas_call(
         functools.partial(kernel, dims, names),
-        out_shape=made,
+        out_shape=tuple(pltpu.VMEM(s.shape, F32) for s in made),
         in_specs=[hbm, hbm, hbm, hbm],
-        out_specs=(hbm, hbm, hbm),
+        out_specs=(vmem, vmem, vmem),
         scratch_shapes=[pltpu.VMEM(shape, F32) for shape in shapes.values()]
         + [
             pltpu.VMEM(codes.shape, jnp.int32),
             pltpu.VMEM(theta.shape, F32),
             pltpu.VMEM(disc.shape, F32),
             pltpu.SMEM(intercept.shape, F32),
-        ]
-        + [pltpu.VMEM(s.shape, F32) for s in made]
-        + [
             pltpu.SemaphoreType.DMA((len(names),)),
             pltpu.SemaphoreType.DMA((len(names),)),
-            pltpu.SemaphoreType.DMA((7,)),
+            pltpu.SemaphoreType.DMA((4,)),
         ],
-        compiler_params=pltpu.CompilerParams(collective_id=0, has_side_effects=True),
-    )(codes, theta, disc, intercept)
+        compiler_params=pltpu.CompilerParams(collective_id=0, has_side_effects=True, vmem_limit_bytes=32 * 2**20),
+    )(*(pltpu.with_memory_space_constraint(a, pltpu.HBM) for a in (codes, theta, disc, intercept)))
     outs = pl.pallas_call(
         hand_over,
-        out_shape=made,
-        in_specs=[hbm, hbm, hbm],
+        out_shape=tuple(pltpu.HBM(s.shape, F32) for s in made),
+        in_specs=[vmem, vmem, vmem],
         out_specs=(hbm, hbm, hbm),
-        scratch_shapes=[pltpu.VMEM(s.shape, F32) for s in made] + [pltpu.SemaphoreType.DMA((6,))],
+        scratch_shapes=[pltpu.SemaphoreType.DMA((3,))],
+        compiler_params=pltpu.CompilerParams(vmem_limit_bytes=2**20),
     )(*outs)
     return outs[0], outs[1], outs[2].reshape(intercept.shape)
 

time: 69.8 us -> 67.3 us (0.964)
  Pallas kernels: 69 us -> 66.5 us
    pallas_call x2, Pallas kernels: 69 us -> 66.5 us  [the longest x1 65.9 us: shards(): pl.pallas_call(functools.partial(kernel, dims, names), out_shape=tuple((p...]
where the time goes in v3:
time: 67.3 us; the launch traced here: 67.2 us
  Pallas kernels  66.5 us (99%)
    pallas_call x1, Pallas kernels, shards(): pl.pallas_call(functools.partial(kernel, dims, names), out_shape=tuple((p...  65.9 us

profile of v3, /device:TPU:1, one launch (start us, length us, event | category | flops | bytes accessed | tf_op | source)
XLA Modules:
  0.0 67.2 jit_solution(16175385810573853866)
XLA Ops:
  0.6 65.9 %shard_map.67 = (f32[8,64]{1,0:T(8,128)S(1)}, f32[8,64]{1,0:T(8,128)S(1)}, f32[1,8]{1,0:T(1,128)S(1)}) custom-call(s32[256,128]{1,0:T(8,128)} %codes_hbm.1, f32[8,64]{1,0:T(8,128)} %theta_hbm.1, f32[8,64]{1,0:T(8,128)} %disc_hbm.1, f32[8]{0:T(128)} %icpt_hbm.1), custom_call_target="tpu_custom_call" | custom-call | tf_op jit(solution)/shard_map/pallas_call | solution.py:413
  66.6 0.6 shard_map.68

commit v4 on v3

--- a/solution.py
+++ b/solution.py
@@ -1,4 +1,5 @@
 import functools
+import math
 
 import jax
 import jax.numpy as jnp
@@ -10,6 +11,8 @@
 DIMS = dict(ZL=4, X=4, ZH=2, Y=8, C=2)
 K = 64
 W = 128
+LOCAL = ("ra1", "ca1", "ra2", "ca2", "xd", "sent")
+SHARED = {"rb2": "rb1", "cb2": "cb1", "sa2": "sa1", "rg1": "t2", "rg2": "t2", "cg1": "d2", "cg2": "d2"}
 MESH = pl.DeviceIdType.MESH
 F32 = jnp.float32
 
@@ -35,10 +38,6 @@
 
 def dot_tn(a, b):
     return dot(a, b, 0, 0)
-
-
-def beside(a, b):
-    return tuple(jnp.concatenate([u, v], 1) for u, v in zip(a, b))
 
 
 def tree_sum(parts):
@@ -48,8 +47,9 @@
     return parts[0]
 
 
-def far_first(count):
-    return sorted(range(1, count), key=lambda k: ({4: 0, 5: 1, 3: 2, 7: 3, 6: 4, 2: 5, 1: 6}.get(k % 8, 7), -k))
+def far_first(count, unit=1):
+    order = {4: 0, 5: 1, 3: 2, 7: 3, 6: 4, 2: 5, 1: 6}
+    return sorted(range(1, count), key=lambda k: (order.get(k // unit % 8, 7), -k))
 
 
 def kernel(dims, names, codes_hbm, theta_hbm, disc_hbm, icpt_hbm, out_t, out_d, out_b, *rest):
@@ -62,21 +62,22 @@
     half = ZL // 2
     zq, zr = zl // half, zl % half
     Q = ZL * X * 8
-    YB, XB = C * 8, half * 8
-    SH = Y * YB
-    NXY, NZC = X * Y, ZL * ZH * C
+    XB = half * 8
+    NYC, NXY, NZC = Y * C, X * Y, ZL * ZH * C
+    SH = NYC * 8
+    yc = y * C + core
 
     def at(zl_, x_, zh_, y_, core_):
         return (zl_ * X + x_, (zh_ * Y + y_) * C + core_)
 
-    def dev_y(k):
-        return at(zl, x, zh, jnp.bitwise_xor(y, k), core)
+    def dev_yc(k):
+        return at(zl, x, zh, jnp.bitwise_xor(y, k // C), jnp.bitwise_xor(core, k % C))
 
     def dev_x(k):
         return at(zl, jnp.bitwise_xor(x, k), zh, y, core)
 
-    def dev_hc(k):
-        return at(zl, x, jnp.bitwise_xor(zh, k // C), y, jnp.bitwise_xor(core, k % C))
+    def dev_h(k):
+        return at(zl, x, jnp.bitwise_xor(zh, k), y, core)
 
     def dev_l(k):
         return at(jnp.bitwise_xor(zl, k), x, zh, y, core)
@@ -89,28 +90,28 @@
             jnp.bitwise_xor(zl, k // (ZH * C)), x, jnp.bitwise_xor(zh, (k // C) % ZH), y, jnp.bitwise_xor(core, k % C)
         )
 
-    index_of = {n: i for i, n in enumerate(names)}
+    serial = sorted({SHARED.get(n, n) for n in names if n not in LOCAL})
+    index_of = {n: serial.index(SHARED.get(n, n)) for n in names if n not in LOCAL}
     sent = []
 
     def send(src, name, slot, device):
+        sent.append(math.prod(src.shape))
         pltpu.make_async_remote_copy(
             src_ref=src,
             dst_ref=ref[name].at[slot],
-            send_sem=ssem.at[index_of[name]],
+            send_sem=ssem,
             recv_sem=rsem.at[index_of[name]],
             device_id=device,
             device_id_type=MESH,
         ).start()
 
-    def spread(name, count, dev):
-        for k in far_first(count):
+    def spread(name, count, dev, unit=1):
+        for k in far_first(count, unit):
             send(ref[name].at[0], name, k, dev(k))
-        sent.append((name, 1, count))
-
-    def scatter(src, name, count, me, dev):
-        for k in far_first(count):
+
+    def scatter(src, name, count, me, dev, unit=1):
+        for k in far_first(count, unit):
             send(ref[src].at[jnp.bitwise_xor(me, k)], name, k - 1, dev(k))
-        sent.append((name, 0, count - 1))
 
     def arrived(name, lo, hi):
         r = ref[name].at[pl.ds(lo, hi - lo)]
@@ -129,7 +130,7 @@
         fetch.start()
 
     barrier = pltpu.get_barrier_semaphore()
-    partners = [dev_y(k) for k in far_first(Y)] + [dev_hc(k) for k in far_first(ZH * C)]
+    partners = [dev_h(1)] + [dev_yc(k) for k in far_first(NYC, C)]
     partners += [dev_l(k) for k in far_first(ZL)] + [dev_x(k) for k in far_first(X)]
     for partner in partners:
         pl.semaphore_signal(barrier, inc=1, device_id=partner, device_id_type=MESH)
@@ -151,7 +152,7 @@
 
     pl.semaphore_wait(barrier, len(partners))
 
-    spread("t1", ZH * C, dev_hc)
+    spread("t1", ZH, dev_h)
     spread("d1", ZL, dev_l)
     spread("b1", ZL, dev_l)
 
@@ -163,14 +164,13 @@
     arrived("b1", 1, ZL)
     ref["b2"][0] = total("b1", ZL)
     spread("b2", X, dev_x)
-    arrived("t1", 1, ZH * C)
-    slot_hc = lambda h, c: jnp.bitwise_xor(zh, h) * C + jnp.bitwise_xor(core, c)
-    t_own = jnp.concatenate([ref["t1"][slot_hc(0, c)] + ref["t1"][slot_hc(1, c)] for c in range(C)], 0)
+    arrived("t1", 1, ZH)
+    t_own = total("t1", ZH)
     ref["t2"][0] = t_own
-    spread("t2", Y, dev_y)
+    spread("t2", NYC, dev_yc, C)
 
     def rows_of(name):
-        return jnp.concatenate([ref[name][jnp.bitwise_xor(y, k)] for k in range(Y)], 0)
+        return jnp.concatenate([ref[name][jnp.bitwise_xor(yc, k)] for k in range(NYC)], 0)
 
     def low(v):
         return lax.broadcasted_iota(jnp.int32, v.shape, 1) < K
@@ -198,7 +198,7 @@
     arrived("b2", 1, X)
     bias = total("b2", X)
     fetches[3].wait()
-    arrived("t2", 1, Y)
+    arrived("t2", 1, NYC)
     theta = rows_of("t2")
     turned = swap(theta)
     lo = low(theta)
@@ -225,8 +225,8 @@
         return jnp.sum(u[0], 0, keepdims=True) + jnp.sum(u[1], 0, keepdims=True)
 
     def put_rows(name, offset, v):
-        for k in range(Y):
-            ref[name][k, pl.ds(offset, YB)] = v[k * YB : (k + 1) * YB]
+        for k in range(NYC):
+            ref[name][k, pl.ds(offset, 8)] = v[k * 8 : (k + 1) * 8]
 
     def put_cols(name, offset, v):
         for k in range(X):
@@ -234,46 +234,49 @@
                 start = (r * X + k) * 8
                 ref[name][k, pl.ds(offset + r * 8, 8)] = v[start : start + 8]
 
-    def reduce_all(tag, row_list, col_list, sums, between=None):
-        for i, v in enumerate(row_list):
-            put_rows("ra" + tag, i * YB, v)
-        scatter("ra" + tag, "rb" + tag, Y, y, dev_y)
-        for i, v in enumerate(col_list):
-            put_cols("ca" + tag, i * XB, v)
+    def reduce_all(tag, row_list, col_list, sums, after_first=None, after_second=None):
+        for i, pair in enumerate(row_list):
+            put_rows("ra" + tag, i * 8, row_part(*pair))
+        scatter("ra" + tag, "rb" + tag, NYC, yc, dev_yc, C)
+        for i, pair in enumerate(col_list):
+            put_cols("ca" + tag, i * XB, col_part(*pair))
         scatter("ca" + tag, "cb" + tag, X, x, dev_x)
-        ref["sa" + tag][0] = sums
+        ref["sa" + tag][0] = jnp.concatenate([col_sum(value) for value in sums], 0)
         spread("sa" + tag, X, dev_x)
+        if after_first is not None:
+            after_first()
         arrived("cb" + tag, 0, X - 1)
         ref["cc" + tag][0] = tree_sum([ref["ca" + tag][x]] + [ref["cb" + tag][k] for k in range(X - 1)])
         spread("cc" + tag, ZL, dev_l)
         arrived("sa" + tag, 1, X)
         ref["sb" + tag][0] = total("sa" + tag, X)
         spread("sb" + tag, ZL, dev_l)
-        arrived("rb" + tag, 0, Y - 1)
-        ref["rc" + tag][0] = tree_sum([ref["ra" + tag][y]] + [ref["rb" + tag][k] for k in range(Y - 1)])
-        spread("rc" + tag, ZH * C, dev_hc)
-        if between is not None:
-            between()
+        arrived("rb" + tag, 0, NYC - 1)
+        ref["rc" + tag][0] = tree_sum([ref["ra" + tag][yc]] + [ref["rb" + tag][k] for k in range(NYC - 1)])
+        spread("rc" + tag, ZH, dev_h)
+        if after_second is not None:
+            after_second()
         arrived("cc" + tag, 1, ZL)
         cols = total("cc" + tag, ZL)
         arrived("sb" + tag, 1, ZL)
         sums = total("sb" + tag, ZL)
-        arrived("rc" + tag, 1, ZH * C)
-        rows = total("rc" + tag, ZH * C)
+        arrived("rc" + tag, 1, ZH)
+        rows = total("rc" + tag, ZH)
         return rows, cols, sums
 
     def gather_start(tag, rows, cols):
         ref["rg" + tag][0] = rows
-        spread("rg" + tag, Y, dev_y)
+        spread("rg" + tag, NYC, dev_yc, C)
         ref["cg" + tag][0] = cols
         spread("cg" + tag, X, dev_x)
 
     def change_of(tag, vb):
         arrived("cg" + tag, 1, X)
         va = cols_of("cg" + tag)
-        arrived("rg" + tag, 1, Y)
-        left = beside(split(rows_of("rg" + tag)), theta_s)
-        return [dot_nt(left, beside(dd_s[h], split(va[h]))) + vb for h in range(ZH)]
+        base = [dot_nt(theta_s, split(va[h])) + vb for h in range(ZH)]
+        arrived("rg" + tag, 1, NYC)
+        vt = split(rows_of("rg" + tag))
+        return [dot_nt(vt, dd_s[h]) + base[h] for h in range(ZH)]
 
     def lanes(v):
         s = jnp.sum(v, 0, keepdims=True)
@@ -282,7 +285,7 @@
         return s
 
     def inner(u, v):
-        rows = lanes(u[0] * v[0]) * (1.0 / (ZH * C))
+        rows = lanes(u[0] * v[0]) * (1.0 / ZH)
         cols = lanes(u[1] * v[1]) * (1.0 / ZL)
         return rows + cols + lanes(u[2] * v[2]) * (1.0 / (ZL * X))
 
@@ -303,30 +306,31 @@
     d2 = [split(d * d) for d in dd]
     t2 = [split(t * t) for t in tt]
     resid_s, weight_s = [split(u) for u in resid], [split(u) for u in weight]
-    sums = jnp.concatenate([col_sum(resid), col_sum(weight)], 0)
     rows, cols, sums = reduce_all(
         "1",
-        (row_part(resid_s, dd_s), row_part(weight_s, d2)),
-        (col_part(resid_s, tt_s), col_part(weight_s, t2)),
-        sums,
+        ((resid_s, dd_s), (weight_s, d2)),
+        ((resid_s, tt_s), (weight_s, t2)),
+        (resid, weight),
     )
-    r = (-(rows[:YB] + t_own), -(cols[:XB] + d_own), -(sums[0:1] + bias))
-    dg = (rows[YB:] + 1.0, cols[XB:] + 1.0, sums[1:2] + 1.0)
+    r = (-(rows[:8] + t_own), -(cols[:XB] + d_own), -(sums[0:1] + bias))
+    dg = (rows[8:] + 1.0, cols[XB:] + 1.0, sums[1:2] + 1.0)
     z = [a / b for a, b in zip(r, dg)]
     gather_start("1", z[0], z[1])
-    rz_part = inner(r, z)
-    zz_part = inner(z, z)
     change = change_of("1", z[2])
     scaled = [w * c for w, c in zip(weight, change)]
     scaled_s = [split(u) for u in scaled]
-    pq_part = lanes(scaled[0] * change[0]) + lanes(scaled[1] * change[1]) + zz_part
-    first_round("1", (rz_part, pq_part))
+
+    def first_scalars():
+        pq_part = lanes(scaled[0] * change[0]) + lanes(scaled[1] * change[1]) + inner(z, z)
+        first_round("1", (inner(r, z), pq_part))
+
     rows, cols, sums = reduce_all(
         "2",
-        (row_part(scaled_s, dd_s),),
-        (col_part(scaled_s, tt_s),),
-        col_sum(scaled),
-        between=lambda: second_round("1"),
+        ((scaled_s, dd_s),),
+        ((scaled_s, tt_s),),
+        (scaled,),
+        first_scalars,
+        lambda: second_round("1"),
     )
     image = (rows + z[0], cols + z[1], sums + z[2])
     scaled_image = [a / b for a, b in zip(image, dg)]
@@ -353,17 +357,14 @@
         (alpha * a + alpha_two * (b + beta * a)) * jnp.sqrt(d) for a, b, d in zip(z, z_next, dg)
     ]
 
-    ref["xt"][...] = step[0]
-    mine = ref["xt"][pl.ds(pl.multiple_of(core * 8, 8), 8)]
-    out_t[...] = jnp.where(zh == 0, mine, swap(mine))[:, :K]
+    out_t[...] = jnp.where(zh == 0, step[0], swap(step[0]))[:, :K]
     ref["xd"][...] = step[1]
     mine = ref["xd"][pl.ds(pl.multiple_of(zr * 8, 8), 8)]
     out_d[...] = jnp.where(zq == 0, mine, swap(mine))[:, :K]
     out_b[...] = pltpu.roll(step[2], lax.rem(Q - stu * 8, Q), 1)[:, :8]
 
-    for name, first, last in sent:
-        like = ref[name].at[pl.ds(first, last - first)]
-        pltpu.make_async_copy(like, like, ssem.at[index_of[name]]).wait()
+    assert sum(sent) == math.prod(ref["sent"].shape)
+    pltpu.make_async_copy(ref["sent"], ref["sent"], ssem).wait()
 
 
 def hand_over(*refs):
@@ -377,27 +378,31 @@
 
 def buffers(dims):
     ZL, X, ZH, Y, C = (dims[n] for n in ("ZL", "X", "ZH", "Y", "C"))
-    Q, YB, XB = ZL * X * 8, C * 8, ZL // 2 * 8
+    Q, NYC, XB = ZL * X * 8, Y * C, ZL // 2 * 8
     shapes = {
-        "t1": (ZH * C, 8, W), "d1": (ZL, 8, W), "b1": (ZL, 1, Q),
-        "t2": (Y, YB, W), "d2": (X, XB, W), "b2": (X, 1, Q),
+        "t1": (ZH, 8, W), "d1": (ZL, 8, W), "b1": (ZL, 1, Q),
+        "t2": (NYC, 8, W), "d2": (X, XB, W), "b2": (X, 1, Q),
     }
     for tag, n in (("1", 2), ("2", 1)):
-        shapes["ra" + tag] = (Y, n * YB, W)
-        shapes["rb" + tag] = (Y - 1, n * YB, W)
-        shapes["rc" + tag] = (ZH * C, n * YB, W)
+        shapes["ra" + tag] = (NYC, n * 8, W)
+        shapes["rb" + tag] = (NYC - 1, n * 8, W)
+        shapes["rc" + tag] = (ZH, n * 8, W)
         shapes["ca" + tag] = (X, n * XB, W)
         shapes["cb" + tag] = (X - 1, n * XB, W)
         shapes["cc" + tag] = (ZL, n * XB, W)
         shapes["sa" + tag] = (X, n, Q)
         shapes["sb" + tag] = (ZL, n, Q)
-        shapes["rg" + tag] = (Y, YB, W)
+        shapes["rg" + tag] = (NYC, 8, W)
         shapes["cg" + tag] = (X, XB, W)
     for tag, n in (("1", 2), ("2", 3)):
         shapes["p" + tag] = (X * Y, n, W)
         shapes["q" + tag] = (ZL * ZH * C, n, W)
-    shapes["xt"] = (YB, W)
+    rows, cols = (NYC - 1) * 8 * W, (X - 1) * XB * W
+    small = (ZH - 1) * 8 * W + (ZL - 1) * XB * W
+    sent = (ZH + ZL - 2) * 8 * W + 6 * (rows + cols) + 3 * small
+    sent += 4 * (ZL + X - 2) * Q + 5 * (X * Y + ZL * ZH * C - 2) * W
     shapes["xd"] = (XB, W)
+    shapes["sent"] = (sent // Q, 1, Q)
     return shapes
 
 
@@ -421,8 +426,8 @@
             pltpu.VMEM(theta.shape, F32),
             pltpu.VMEM(disc.shape, F32),
             pltpu.SMEM(intercept.shape, F32),
-            pltpu.SemaphoreType.DMA((len(names),)),
-            pltpu.SemaphoreType.DMA((len(names),)),
+            pltpu.SemaphoreType.DMA,
+            pltpu.SemaphoreType.DMA((len(names) - len(LOCAL) - len(SHARED),)),
             pltpu.SemaphoreType.DMA((4,)),
         ],
         compiler_params=pltpu.CompilerParams(collective_id=0, has_side_effects=True, vmem_limit_bytes=32 * 2**20),

time: 67.3 us -> 66.2 us (0.984)
  Pallas kernels: 66.5 us -> 65.4 us
    pallas_call x1, Pallas kernels: 65.9 us -> 64.8 us  [shards(): pl.pallas_call(functools.partial(kernel, dims, names), out_shape=tuple((p...]
where the time goes in v4:
time: 66.2 us; the launch traced here: 66.1 us
  Pallas kernels  65.4 us (99%)
    pallas_call x1, Pallas kernels, shards(): pl.pallas_call(functools.partial(kernel, dims, names), out_shape=tuple((p...  64.8 us

profile of v4, /device:TPU:1, one launch (start us, length us, event | category | flops | bytes accessed | tf_op | source)
XLA Modules:
  0.0 66.1 jit_solution(1665638140416556409)
XLA Ops:
  0.6 64.8 %shard_map.67 = (f32[8,64]{1,0:T(8,128)S(1)}, f32[8,64]{1,0:T(8,128)S(1)}, f32[1,8]{1,0:T(1,128)S(1)}) custom-call(s32[256,128]{1,0:T(8,128)} %codes_hbm.1, f32[8,64]{1,0:T(8,128)} %theta_hbm.1, f32[8,64]{1,0:T(8,128)} %disc_hbm.1, f32[8]{0:T(128)} %icpt_hbm.1), custom_call_target="tpu_custom_call" | custom-call | tf_op jit(solution)/shard_map/pallas_call | solution.py:418
  65.4 0.6 shard_map.68

commit v5 on v4

--- a/solution.py
+++ b/solution.py
@@ -50,6 +50,12 @@
 def far_first(count, unit=1):
     order = {4: 0, 5: 1, 3: 2, 7: 3, 6: 4, 2: 5, 1: 6}
     return sorted(range(1, count), key=lambda k: (order.get(k // unit % 8, 7), -k))
+
+
+Y_HOPS, X_HOPS = (0, 1, 2, 2, 4, 3, 2, 2), (0, 1, 2, 1)
+PLANE = sorted(range(1, 32), key=lambda k: -Y_HOPS[k % 8] - X_HOPS[k // 8])
+Z_HOPS = (0, 1, 2, 2, 4, 3, 2, 2)
+LINE = sorted(range(1, 16), key=lambda k: -Z_HOPS[k // 2 % 2 * 4 + k // 4] - 0.5 * (k % 2))
 
 
 def kernel(dims, names, codes_hbm, theta_hbm, disc_hbm, icpt_hbm, out_t, out_d, out_b, *rest):
@@ -76,6 +82,11 @@
     def dev_x(k):
         return at(zl, jnp.bitwise_xor(x, k), zh, y, core)
 
+    def dev_q(k):
+        return at(
+            zl, x, jnp.bitwise_xor(zh, k // NYC), jnp.bitwise_xor(y, k // C % Y), jnp.bitwise_xor(core, k % C)
+        )
+
     def dev_h(k):
         return at(zl, x, jnp.bitwise_xor(zh, k), y, core)
 
@@ -234,10 +245,14 @@
                 start = (r * X + k) * 8
                 ref[name][k, pl.ds(offset + r * 8, 8)] = v[start : start + 8]
 
-    def reduce_all(tag, row_list, col_list, sums, after_first=None, after_second=None):
+    def reduce_all(tag, row_list, col_list, sums, direct=False, after_first=None, after_second=None):
         for i, pair in enumerate(row_list):
             put_rows("ra" + tag, i * 8, row_part(*pair))
-        scatter("ra" + tag, "rb" + tag, NYC, yc, dev_yc, C)
+        if direct:
+            for k in [NYC + k for k in far_first(NYC, C) + [0]] + far_first(NYC, C):
+                send(ref["ra" + tag].at[jnp.bitwise_xor(yc, k % NYC)], "rb" + tag, k - 1, dev_q(k))
+        else:
+            scatter("ra" + tag, "rb" + tag, NYC, yc, dev_yc, C)
         for i, pair in enumerate(col_list):
             put_cols("ca" + tag, i * XB, col_part(*pair))
         scatter("ca" + tag, "cb" + tag, X, x, dev_x)
@@ -251,17 +266,26 @@
         arrived("sa" + tag, 1, X)
         ref["sb" + tag][0] = total("sa" + tag, X)
         spread("sb" + tag, ZL, dev_l)
-        arrived("rb" + tag, 0, NYC - 1)
-        ref["rc" + tag][0] = tree_sum([ref["ra" + tag][yc]] + [ref["rb" + tag][k] for k in range(NYC - 1)])
-        spread("rc" + tag, ZH, dev_h)
+        senders = ZH * NYC - 1 if direct else NYC - 1
+
+        def row_total():
+            arrived("rb" + tag, 0, senders)
+            return tree_sum([ref["ra" + tag][yc]] + [ref["rb" + tag][k] for k in range(senders)])
+
+        if not direct:
+            ref["rc" + tag][0] = row_total()
+            spread("rc" + tag, ZH, dev_h)
         if after_second is not None:
             after_second()
         arrived("cc" + tag, 1, ZL)
         cols = total("cc" + tag, ZL)
         arrived("sb" + tag, 1, ZL)
         sums = total("sb" + tag, ZL)
-        arrived("rc" + tag, 1, ZH)
-        rows = total("rc" + tag, ZH)
+        if direct:
+            rows = row_total()
+        else:
+            arrived("rc" + tag, 1, ZH)
+            rows = total("rc" + tag, ZH)
         return rows, cols, sums
 
     def gather_start(tag, rows, cols):
@@ -289,19 +313,28 @@
         cols = lanes(u[1] * v[1]) * (1.0 / ZL)
         return rows + cols + lanes(u[2] * v[2]) * (1.0 / (ZL * X))
 
+    def own_lanes(count):
+        group = lax.broadcasted_iota(jnp.int32, (count, W), 1) // 32
+        return group == lax.broadcasted_iota(jnp.int32, (count, W), 0)
+
     def first_round(tag, values):
-        for i, v in enumerate(values):
-            ref["p" + tag][0, pl.ds(i, 1)] = v
-        spread("p" + tag, NXY, dev_xy)
+        stacked = jnp.concatenate(values, 0)
+        stacked = stacked + pltpu.roll(stacked, 64, 1)
+        stacked = stacked + pltpu.roll(stacked, 32, 1)
+        ref["p" + tag][0] = jnp.sum(jnp.where(own_lanes(len(values)), stacked, 0.0), 0, keepdims=True)
+        for k in PLANE if NXY == 32 else range(1, NXY):
+            send(ref["p" + tag].at[0], "p" + tag, k, dev_xy(k))
 
     def second_round(tag):
         arrived("p" + tag, 1, NXY)
         ref["q" + tag][0] = jnp.sum(ref["p" + tag][...], 0)
-        spread("q" + tag, NZC, dev_zc)
-
-    def last_round(tag):
+        for k in LINE if NZC == 16 else range(1, NZC):
+            send(ref["q" + tag].at[0], "q" + tag, k, dev_zc(k))
+
+    def last_round(tag, count):
         arrived("q" + tag, 1, NZC)
-        return jnp.sum(jnp.sum(ref["q" + tag][...], 0), 1, keepdims=True)
+        row = jnp.sum(ref["q" + tag][...], 0)
+        return jnp.sum(jnp.where(own_lanes(count), row, 0.0), 1, keepdims=True)
 
     d2 = [split(d * d) for d in dd]
     t2 = [split(t * t) for t in tt]
@@ -329,13 +362,14 @@
         ((scaled_s, dd_s),),
         ((scaled_s, tt_s),),
         (scaled,),
-        first_scalars,
-        lambda: second_round("1"),
+        direct=True,
+        after_first=first_scalars,
+        after_second=lambda: second_round("1"),
     )
     image = (rows + z[0], cols + z[1], sums + z[2])
     scaled_image = [a / b for a, b in zip(image, dg)]
     gather_start("2", scaled_image[0], scaled_image[1])
-    scalars = last_round("1")
+    scalars = last_round("1", 2)
     rz, pq = scalars[0:1], scalars[1:2]
     alpha = rz / pq
     r = [a - alpha * b for a, b in zip(r, image)]
@@ -349,7 +383,7 @@
         cross_part = cross_part + lanes(wn * c)
     first_round("2", (new_part, own_part, cross_part))
     second_round("2")
-    scalars = last_round("2")
+    scalars = last_round("2", 3)
     new, own, cross = scalars[0:1], scalars[1:2], scalars[2:3]
     beta = new / rz
     alpha_two = new / (own + 2.0 * beta * cross + beta * beta * pq)
@@ -385,8 +419,9 @@
     }
     for tag, n in (("1", 2), ("2", 1)):
         shapes["ra" + tag] = (NYC, n * 8, W)
-        shapes["rb" + tag] = (NYC - 1, n * 8, W)
-        shapes["rc" + tag] = (ZH, n * 8, W)
+        shapes["rb" + tag] = ((NYC if n == 2 else ZH * NYC) - 1, n * 8, W)
+        if n == 2:
+            shapes["rc" + tag] = (ZH, n * 8, W)
         shapes["ca" + tag] = (X, n * XB, W)
         shapes["cb" + tag] = (X - 1, n * XB, W)
         shapes["cc" + tag] = (ZL, n * XB, W)
@@ -394,13 +429,13 @@
         shapes["sb" + tag] = (ZL, n, Q)
         shapes["rg" + tag] = (NYC, 8, W)
         shapes["cg" + tag] = (X, XB, W)
-    for tag, n in (("1", 2), ("2", 3)):
-        shapes["p" + tag] = (X * Y, n, W)
-        shapes["q" + tag] = (ZL * ZH * C, n, W)
+    for tag in ("1", "2"):
+        shapes["p" + tag] = (X * Y, 1, W)
+        shapes["q" + tag] = (ZL * ZH * C, 1, W)
     rows, cols = (NYC - 1) * 8 * W, (X - 1) * XB * W
     small = (ZH - 1) * 8 * W + (ZL - 1) * XB * W
-    sent = (ZH + ZL - 2) * 8 * W + 6 * (rows + cols) + 3 * small
-    sent += 4 * (ZL + X - 2) * Q + 5 * (X * Y + ZL * ZH * C - 2) * W
+    sent = (ZH + ZL - 2) * 8 * W + 7 * rows + 6 * cols + 3 * small
+    sent += 4 * (ZL + X - 2) * Q + 2 * (X * Y + ZL * ZH * C - 2) * W
     shapes["xd"] = (XB, W)
     shapes["sent"] = (sent // Q, 1, Q)
     return shapes

time: 66.2 us -> 64.8 us (0.979)
  Pallas kernels: 65.4 us -> 64 us
    pallas_call x1, Pallas kernels: 64.8 us -> 63.3 us  [shards(): pl.pallas_call(functools.partial(kernel, dims, names), out_shape=tuple((p...]
where the time goes in v5:
time: 64.8 us; the launch traced here: 64.6 us
  Pallas kernels  64 us (99%)
    pallas_call x1, Pallas kernels, shards(): pl.pallas_call(functools.partial(kernel, dims, names), out_shape=tuple((p...  63.3 us

profile of v5, /device:TPU:1, one launch (start us, length us, event | category | flops | bytes accessed | tf_op | source)
XLA Modules:
  0.0 64.6 jit_solution(2999287723850534707)
XLA Ops:
  0.6 63.3 %shard_map.67 = (f32[8,64]{1,0:T(8,128)S(1)}, f32[8,64]{1,0:T(8,128)S(1)}, f32[1,8]{1,0:T(1,128)S(1)}) custom-call(s32[256,128]{1,0:T(8,128)} %codes_hbm.1, f32[8,64]{1,0:T(8,128)} %theta_hbm.1, f32[8,64]{1,0:T(8,128)} %disc_hbm.1, f32[8]{0:T(128)} %icpt_hbm.1), custom_call_target="tpu_custom_call" | custom-call | tf_op jit(solution)/shard_map/pallas_call | solution.py:453
  64.0 0.6 shard_map.68

commit v6 on v5

--- a/solution.py
+++ b/solution.py
@@ -167,6 +167,10 @@
     spread("d1", ZL, dev_l)
     spread("b1", ZL, dev_l)
 
+    arrived("t1", 1, ZH)
+    t_own = total("t1", ZH)
+    ref["t2"][0] = t_own
+    spread("t2", NYC, dev_yc, C)
     arrived("d1", 1, ZL)
     slot_l = lambda z: jnp.bitwise_xor(zl, z)
     d_own = jnp.concatenate([ref["d1"][slot_l(r)] + ref["d1"][slot_l(half + r)] for r in range(half)], 0)
@@ -175,10 +179,6 @@
     arrived("b1", 1, ZL)
     ref["b2"][0] = total("b1", ZL)
     spread("b2", X, dev_x)
-    arrived("t1", 1, ZH)
-    t_own = total("t1", ZH)
-    ref["t2"][0] = t_own
-    spread("t2", NYC, dev_yc, C)
 
     def rows_of(name):
         return jnp.concatenate([ref[name][jnp.bitwise_xor(yc, k)] for k in range(NYC)], 0)
@@ -382,20 +382,29 @@
         own_part = own_part + lanes(wn * n)
         cross_part = cross_part + lanes(wn * c)
     first_round("2", (new_part, own_part, cross_part))
+
+    root = [jnp.sqrt(d) for d in dg]
+
+    def own_parts(i, p):
+        scaled_p = [a * b for a, b in zip(p, root)]
+        ref["xd"][i] = scaled_p[1]
+        mine = ref["xd"][i, pl.ds(pl.multiple_of(zr * 8, 8), 8)]
+        return (
+            jnp.where(zh == 0, scaled_p[0], swap(scaled_p[0])),
+            jnp.where(zq == 0, mine, swap(mine)),
+            pltpu.roll(scaled_p[2], lax.rem(Q - stu * 8, Q), 1),
+        )
+
+    parts = list(zip(own_parts(0, z), own_parts(1, z_next)))
     second_round("2")
     scalars = last_round("2", 3)
     new, own, cross = scalars[0:1], scalars[1:2], scalars[2:3]
     beta = new / rz
     alpha_two = new / (own + 2.0 * beta * cross + beta * beta * pq)
-    step = [
-        (alpha * a + alpha_two * (b + beta * a)) * jnp.sqrt(d) for a, b, d in zip(z, z_next, dg)
-    ]
-
-    out_t[...] = jnp.where(zh == 0, step[0], swap(step[0]))[:, :K]
-    ref["xd"][...] = step[1]
-    mine = ref["xd"][pl.ds(pl.multiple_of(zr * 8, 8), 8)]
-    out_d[...] = jnp.where(zq == 0, mine, swap(mine))[:, :K]
-    out_b[...] = pltpu.roll(step[2], lax.rem(Q - stu * 8, Q), 1)[:, :8]
+    steps = [alpha * a + alpha_two * (b + beta * a) for a, b in parts]
+    out_t[...] = steps[0][:, :K]
+    out_d[...] = steps[1][:, :K]
+    out_b[...] = steps[2][:, :8]
 
     assert sum(sent) == math.prod(ref["sent"].shape)
     pltpu.make_async_copy(ref["sent"], ref["sent"], ssem).wait()
@@ -436,7 +445,7 @@
     small = (ZH - 1) * 8 * W + (ZL - 1) * XB * W
     sent = (ZH + ZL - 2) * 8 * W + 7 * rows + 6 * cols + 3 * small
     sent += 4 * (ZL + X - 2) * Q + 2 * (X * Y + ZL * ZH * C - 2) * W
-    shapes["xd"] = (XB, W)
+    shapes["xd"] = (2, XB, W)
     shapes["sent"] = (sent // Q, 1, Q)
     return shapes
 

time: 64.8 us -> 64.7 us (level)
  no operation moved by 1% of the time
where the time goes in v6:
time: 64.7 us; the launch traced here: 64.5 us
  Pallas kernels  63.9 us (99%)
    pallas_call x1, Pallas kernels, shards(): pl.pallas_call(functools.partial(kernel, dims, names), out_shape=tuple((p...  63.3 us

profile of v6, /device:TPU:1, one launch (start us, length us, event | category | flops | bytes accessed | tf_op | source)
XLA Modules:
  0.0 64.5 jit_solution(10149428673838687362)
XLA Ops:
  0.6 63.3 %shard_map.67 = (f32[8,64]{1,0:T(8,128)S(1)}, f32[8,64]{1,0:T(8,128)S(1)}, f32[1,8]{1,0:T(1,128)S(1)}) custom-call(s32[256,128]{1,0:T(8,128)} %codes_hbm.1, f32[8,64]{1,0:T(8,128)} %theta_hbm.1, f32[8,64]{1,0:T(8,128)} %disc_hbm.1, f32[8]{0:T(128)} %icpt_hbm.1), custom_call_target="tpu_custom_call" | custom-call | tf_op jit(solution)/shard_map/pallas_call | solution.py:462
  63.9 0.6 shard_map.68

commit v7 on v6

--- a/solution.py
+++ b/solution.py
@@ -141,8 +141,11 @@
         fetch.start()
 
     barrier = pltpu.get_barrier_semaphore()
-    partners = [dev_h(1)] + [dev_yc(k) for k in far_first(NYC, C)]
-    partners += [dev_l(k) for k in far_first(ZL)] + [dev_x(k) for k in far_first(X)]
+    near_y = [dev_yc(k) for k in far_first(NYC, C)]
+    near_l = [dev_l(k) for k in far_first(ZL)]
+    far = 3 * C
+    partners = [dev_h(1)] + near_y[:far] + near_l + near_y[far : 2 * far]
+    partners += [dev_x(k) for k in far_first(X)] + near_y[2 * far :]
     for partner in partners:
         pl.semaphore_signal(barrier, inc=1, device_id=partner, device_id_type=MESH)
     fetches[3].start()

time: 64.7 us -> 64.8 us (level)
  no operation moved by 1% of the time
where the time goes in v7:
time: 64.8 us; the launch traced here: 64.7 us
  Pallas kernels  64 us (99%)
    pallas_call x1, Pallas kernels, shards(): pl.pallas_call(functools.partial(kernel, dims, names), out_shape=tuple((p...  63.4 us

profile of v7, /device:TPU:1, one launch (start us, length us, event | category | flops | bytes accessed | tf_op | source)
XLA Modules:
  0.0 64.7 jit_solution(17201163756597145299)
XLA Ops:
  0.6 63.4 %shard_map.67 = (f32[8,64]{1,0:T(8,128)S(1)}, f32[8,64]{1,0:T(8,128)S(1)}, f32[1,8]{1,0:T(1,128)S(1)}) custom-call(s32[256,128]{1,0:T(8,128)} %codes_hbm.1, f32[8,64]{1,0:T(8,128)} %theta_hbm.1, f32[8,64]{1,0:T(8,128)} %disc_hbm.1, f32[8]{0:T(128)} %icpt_hbm.1), custom_call_target="tpu_custom_call" | custom-call | tf_op jit(solution)/shard_map/pallas_call | solution.py:465
  64.0 0.6 shard_map.68
